TPU v7x, 256 devices: a whole 4x4x8 slice. The times are simulated.
256 devices in a mesh: expert: 64 (over y, z_hi, x, core), hidden: 4 (over z_lo).
Axes of the slice: x: 4, y: 4, z: 8 (z_hi: 2, z_lo: 4; z = z_hi * 4 + z_lo), core: 2. Of those that a mesh axis runs over, the one named last changes fastest.
Arguments:
- tokens: bfloat16 [50176, 768], P(('expert', 'hidden')), may hold values from -512 to 512
- out_grad: bfloat16 [50176, 768], P(('expert', 'hidden')), may hold values from -12 to 12
- slot_router: bfloat16 [768, 256], replicated, may hold values from -0.5 to 0.5
- weight_in: bfloat16 [128, 768, 3072], P('expert', None, 'hidden'), may hold values from -0.21875 to 0.21875
- weight_out: bfloat16 [128, 3072, 768], P('expert', 'hidden'), may hold values from -0.109375 to 0.109375
Outputs:
- token_grad: bfloat16 [50176, 768], P(('expert', 'hidden'))
- router_grad: float32 [768, 256], P('hidden', 'expert')
- weight_in_grad: bfloat16 [128, 768, 3072], P('expert', None, 'hidden')
- weight_out_grad: bfloat16 [128, 3072, 768], P('expert', 'hidden')
All inputs are finite; a program needn't handle non-finite values.
Results may differ from a plain program's by a relative error of at most 0.019.
Values may be sent and summed in bfloat16 or wider, within the bound.
A program may use at most 64 MiB of HBM per device.

v0:
```python
import jax
import jax.numpy as jnp
from jax import lax
from jax.sharding import PartitionSpec as P

D = 768
SLOTS = 2
TOK = 196


def gelu_value(values):
    return 0.5 * values * (1.0 + lax.erf(values * 0.7071067811865476))


def gelu_slope(values):
    return (
        0.5 * (1.0 + lax.erf(values * 0.7071067811865476))
        + values * jnp.exp(-0.5 * values * values) * 0.3989422804014327
    )


def to_experts(stacked_slots):
    crossed = lax.all_to_all(stacked_slots, "expert", split_axis=2, concat_axis=0, tiled=True)
    arrived = lax.all_gather(crossed, "hidden", axis=0, tiled=True)
    return arrived


def to_owners(partials):
    rounded = lax.optimization_barrier(partials.astype(jnp.bfloat16))
    summed = lax.psum_scatter(
        rounded.astype(jnp.float32).astype(jnp.bfloat16), "hidden", scatter_dimension=0, tiled=True
    )
    result = lax.all_to_all(summed, "expert", split_axis=0, concat_axis=2, tiled=True)
    return result


def per_device(tokens, out_grad, slot_router, weight_in, weight_out):
    images = tokens.shape[0] // TOK
    local_experts = weight_in.shape[0]
    inputs = tokens.reshape(images, TOK, D)
    out_grads = out_grad.reshape(images, TOK, D)
    logits = jnp.einsum("btd,dc->btc", inputs, slot_router, preferred_element_type=jnp.float32)
    dispatch = jax.nn.softmax(logits, axis=1)
    combine = jax.nn.softmax(logits, axis=2)
    dispatch16 = dispatch.astype(jnp.bfloat16)
    combine16 = combine.astype(jnp.bfloat16)
    slot_in = jnp.einsum(
        "btc,btd->bcd", dispatch16, inputs, preferred_element_type=jnp.float32
    ).astype(jnp.bfloat16)
    slot_grad = jnp.einsum(
        "btc,btd->bcd", combine16, out_grads, preferred_element_type=jnp.float32
    ).astype(jnp.bfloat16)
    arrived = to_experts(slot_in[:, None])
    received = arrived[:, 0]
    row_count = received.shape[0]
    slot_inputs = received.reshape(row_count, local_experts, SLOTS, D)
    pre_act = jnp.einsum(
        "resd,edf->resf", slot_inputs, weight_in, preferred_element_type=jnp.float32
    )
    activated = gelu_value(pre_act).astype(jnp.bfloat16)
    partial_value = jnp.einsum(
        "resf,efd->resd", activated, weight_out, preferred_element_type=jnp.float32
    )
    slot_inputs, pre_act, activated, forward_part = (
        slot_inputs,
        pre_act,
        activated,
        partial_value.reshape(row_count, 1, local_experts * SLOTS, D),
    )
    slot_out = to_owners(forward_part)[:, 0]
    arrived_grad = to_experts(slot_grad[:, None])
    received_grad = arrived_grad[:, 0]
    row_count = received_grad.shape[0]
    slot_grads = received_grad.reshape(row_count, local_experts, SLOTS, D)
    d_act = jnp.einsum("resd,efd->resf", slot_grads, weight_out, preferred_element_type=jnp.float32)
    d_pre = (d_act * gelu_slope(pre_act)).astype(jnp.bfloat16)
    grad_second = jnp.einsum(
        "resf,resd->efd", activated, slot_grads, preferred_element_type=jnp.float32
    ).astype(jnp.bfloat16)
    grad_first = jnp.einsum(
        "resd,resf->edf", slot_inputs, d_pre, preferred_element_type=jnp.float32
    ).astype(jnp.bfloat16)
    partial_value = jnp.einsum(
        "resf,edf->resd", d_pre, weight_in, preferred_element_type=jnp.float32
    )
    backward_part = partial_value.reshape(row_count, 1, local_experts * SLOTS, D)
    slot_in_grad = to_owners(backward_part)[:, 0]
    d_combine = jnp.einsum("btd,bcd->btc", out_grads, slot_out, preferred_element_type=jnp.float32)
    d_dispatch = jnp.einsum(
        "btd,bcd->btc", inputs, slot_in_grad, preferred_element_type=jnp.float32
    )
    from_combine = combine * (d_combine - jnp.sum(combine * d_combine, axis=2, keepdims=True))
    from_dispatch = dispatch * (d_dispatch - jnp.sum(dispatch * d_dispatch, axis=1, keepdims=True))
    d_logits = (from_combine + from_dispatch).astype(jnp.bfloat16)
    token_grad = (
        jnp.einsum("btc,bcd->btd", dispatch16, slot_in_grad, preferred_element_type=jnp.float32)
        + jnp.einsum("btc,dc->btd", d_logits, slot_router, preferred_element_type=jnp.float32)
    ).astype(jnp.bfloat16)
    router_term = jnp.einsum("btd,btc->dc", inputs, d_logits, preferred_element_type=jnp.float32)
    router_sum = lax.psum(router_term, ("expert", "hidden"))
    row_count = router_term.shape[0] // lax.axis_size("hidden")
    col_count = router_term.shape[1] // lax.axis_size("expert")
    router_grad = lax.dynamic_slice(
        router_sum,
        (lax.axis_index("hidden") * row_count, lax.axis_index("expert") * col_count),
        (row_count, col_count),
    )
    return (token_grad.reshape(images * TOK, D), router_grad, grad_first, grad_second)


def solution(mesh):
    return jax.shard_map(
        per_device,
        mesh=mesh,
        in_specs=(
            P(("expert", "hidden"), None),
            P(("expert", "hidden"), None),
            P(),
            P("expert", None, "hidden"),
            P("expert", "hidden", None),
        ),
        out_specs=(
            P(("expert", "hidden"), None),
            P("hidden", "expert"),
            P("expert", None, "hidden"),
            P("expert", "hidden", None),
        ),
        check_vma=False,
    )
```

profile of v0, /device:TPU:1, one launch (start us, length us, event | category | flops | bytes accessed | tf_op | source)
XLA Modules:
  0.0 541.1 jit_solution(13264223133541740712)
XLA Ops:
  7.2 0.0 copy-start
  7.2 0.0 all-gather.5.cloned.1.call-start
  7.2 1.6 fusion.40
  8.8 0.2 fusion.32
  9.0 1.3 fusion.28
  10.3 0.6 copy.63
  10.9 0.5 broadcast.44
  11.4 3.9 reduce.16
  15.3 1.2 reshape.157
  16.5 30.6 %all_to_all.42 = bf16[64,2,1536]{2,1,0:T(2,128)(2,1)} all-to-all(bf16[64,2,1536]{2,1,0:T(2,128)(2,1)S(1)} %reshape.157), channel_id=1, replica_groups=mesh['expert'=64,'hidden'=4] {'expert'}, dimensions={0} | all-to-all | bytes 786432 | tf_op jit(solution)/shard_map/all_to_all | solution.py:23
  47.1 2.7 reshape.158
  49.9 3.0 bitcast_reduce_fusion.1
  52.9 1.8 all_to_all.15
  54.7 0.0 all-gather.5.cloned.1.call-update
  54.7 0.2 all-gather.3.cloned.1.call-start
  55.0 1.4 fusion.27
  56.3 0.6 copy.64
  57.0 3.9 reduce.17
  60.8 1.2 reshape.159
  62.1 26.6 %all_to_all.43 = bf16[64,2,1536]{2,1,0:T(2,128)(2,1)} all-to-all(bf16[64,2,1536]{2,1,0:T(2,128)(2,1)S(1)} %reshape.159), channel_id=1, replica_groups=mesh['expert'=64,'hidden'=4] {'expert'}, dimensions={0} | all-to-all | bytes 786432 | tf_op jit(solution)/shard_map/all_to_all | solution.py:23
  88.6 2.7 reshape.160
  91.4 3.0 bitcast_reduce_fusion
  94.4 1.9 all_to_all.13
  96.3 0.0 all-gather.3.cloned.1.call-update
  96.3 0.3 reduce-scatter.9.cloned.1.call-start
  96.6 5.8 %all-gather.5.cloned.1.call-done = bf16[256,1,4,768]{3,2,1,0:T(4,128)(2,1)} async-done(((bf16[64,1,4,768]{3,2,1,0:T(4,128)(2,1)}), bf16[256,1,4,768]{3,2,1,0:T(4,128)(2,1)}) %all-gather.5.cloned.1.call-update) | async-done | bytes 1572880 | tf_op jit(solution)/shard_map/all_gather | solution.py:24
  102.4 1.6 copy.36
  104.0 1.1 copy-done.2
  105.1 3.0 fusion.9
  108.2 37.1 %all-gather.3.cloned.1.call-done = bf16[256,1,4,768]{3,2,1,0:T(4,128)(2,1)} async-done(((bf16[64,1,4,768]{3,2,1,0:T(4,128)(2,1)}), bf16[256,1,4,768]{3,2,1,0:T(4,128)(2,1)}) %all-gather.3.cloned.1.call-update) | async-done | bytes 1572880 | tf_op jit(solution)/shard_map/all_gather | solution.py:24
  145.3 1.8 copy.33
  147.0 0.4 copy-done.7
  147.4 3.8 fusion.5
  151.2 1.4 fusion.21
  152.6 1.2 copy.51
  153.8 1.4 copy.59
  155.3 0.0 reduce-scatter.9.cloned.1.call-update
  155.3 0.0 reduce-scatter.11.cloned.1.call-start
  155.3 3.5 fusion.18
  158.9 1.2 copy.53
  160.1 1.4 copy.60
  161.5 0.0 reduce-scatter.11.cloned.1.call-update
  161.6 34.0 %reduce-scatter.9.cloned.1.call-done = bf16[64,3072]{1,0:T(8,128)(2,1)} async-done(((bf16[256,3072]{1,0:T(8,128)(2,1)}), bf16[64,3072]{1,0:T(8,128)(2,1)}) %reduce-scatter.9.cloned.1.call-update) | async-done | bytes 393232
  195.6 2.0 reshape.152
  197.6 11.4 %all-to-all-start.2 = ((bf16[64,1,4,768]{3,2,1,0:T(4,128)(2,1)}), bf16[64,1,4,768]{3,2,1,0:T(4,128)(2,1)S(1)}, u32[]{:S(2)}, u32[]{:S(2)}) async-start(bf16[64,1,4,768]{3,2,1,0:T(4,128)(2,1)} %reshape.152), calls=%async_computation.2 | async-start | bytes 786432 | tf_op jit(solution)/shard_map/all_to_all | solution.py:33
  209.0 37.6 %reduce-scatter.11.cloned.1.call-done = bf16[64,3072]{1,0:T(8,128)(2,1)} async-done(((bf16[256,3072]{1,0:T(8,128)(2,1)}), bf16[64,3072]{1,0:T(8,128)(2,1)}) %reduce-scatter.11.cloned.1.call-update) | async-done | bytes 393232
  246.6 2.0 reshape.154
  248.6 11.2 %all-to-all-start.3 = ((bf16[64,1,4,768]{3,2,1,0:T(4,128)(2,1)}), bf16[64,1,4,768]{3,2,1,0:T(4,128)(2,1)}, u32[]{:S(2)}, u32[]{:S(2)}) async-start(bf16[64,1,4,768]{3,2,1,0:T(4,128)(2,1)} %reshape.154), calls=%async_computation.3 | async-start | bytes 786432 | tf_op jit(solution)/shard_map/all_to_all | solution.py:33
  259.8 0.3 all-reduce.2.cloned.1.call-start
  260.1 4.9 bitcast_convert_fusion
  265.0 0.0 copy-start.1
  265.0 2.9 bitcast_convert_fusion.1
  267.9 1.1 reshape.145
  269.0 0.3 convolution_bitcast_fusion.1
  269.3 7.3 %all-to-all-done.3 = bf16[64,1,4,768]{3,2,1,0:T(4,128)(2,1)} async-done(((bf16[64,1,4,768]{3,2,1,0:T(4,128)(2,1)}), bf16[64,1,4,768]{3,2,1,0:T(4,128)(2,1)}, u32[]{:S(2)}, u32[]{:S(2)}) %all-to-all-start.3) | async-done | bytes 393248 | tf_op jit(solution)/shard_map/all_to_all | solution.py:33
  276.6 1.8 reshape.146
  278.5 1.5 multiply_reduce_fusion.1
  279.9 1.1 add_convert_fusion
  281.0 1.2 convolution_bitcast_fusion
  282.2 0.0 all-reduce.2.cloned.1.call-update
  282.3 0.3 fusion.34
  282.5 2.0 fusion.26
  284.6 248.7 %all-reduce.2.cloned.1.call-done = f32[768,256]{0,1:T(8,128)} async-done(((f32[768,256]{0,1:T(8,128)}), f32[768,256]{0,1:T(8,128)}) %all-reduce.2.cloned.1.call-update) | async-done | bytes 786448 | tf_op jit(solution)/shard_map/psum | solution.py:100
  533.2 1.4 dynamic_slice.3
  (17 shorter events, 0.0 us)
Async XLA Ops:
  7.2 98.0 %copy-start = (bf16[2,768,768]{2,1,0:T(8,128)(2,1)S(1)}, bf16[2,768,768]{2,1,0:T(8,128)(2,1)}, u32[]{:S(2)}) copy-start(bf16[2,768,768]{2,1,0:T(8,128)(2,1)} %param.8) | copy-start | bytes 7077892
  7.2 95.2 %all-gather.5.cloned.1.call-start = ((), (), s32[]{:S(2)}) async-start(), calls=%async_computation.7 | async-start | bytes 1966080 | tf_op jit(solution)/shard_map/all_gather | solution.py:24
  54.7 90.5 %all-gather.3.cloned.1.call-start = ((), (), s32[]{:S(2)}) async-start(), calls=%async_computation.6 | async-start | bytes 1966080 | tf_op jit(solution)/shard_map/all_gather | solution.py:24
  96.3 99.3 %reduce-scatter.9.cloned.1.call-start = ((), (), s32[]{:S(2)}) async-start(), calls=%async_computation.9 | async-start | bytes 1966080
  104.0 1.1 copy-start.2
  145.3 2.1 copy-start.7
  147.0 4.1 copy-start.4
  151.2 1.4 copy-start.8
  155.3 91.3 %reduce-scatter.11.cloned.1.call-start = ((), (), s32[]{:S(2)}) async-start(), calls=%async_computation.10 | async-start | bytes 1966080
  197.6 51.0 %all-to-all-start.2 = ((bf16[64,1,4,768]{3,2,1,0:T(4,128)(2,1)}), bf16[64,1,4,768]{3,2,1,0:T(4,128)(2,1)S(1)}, u32[]{:S(2)}, u32[]{:S(2)}) async-start(bf16[64,1,4,768]{3,2,1,0:T(4,128)(2,1)} %reshape.152), calls=%async_computation.2 | async-start | bytes 786432 | tf_op jit(solution)/shard_map/all_to_all | solution.py:33
  248.6 16.4 %copy-start.5 = (bf16[64,1,4,768]{3,2,1,0:T(4,128)(2,1)}, bf16[64,1,4,768]{3,2,1,0:T(4,128)(2,1)S(1)}, u32[]{:S(2)}) copy-start(bf16[64,1,4,768]{3,2,1,0:T(4,128)(2,1)S(1)} %all-to-all-done.2) | copy-start | bytes 1179652
  248.6 28.0 %all-to-all-start.3 = ((bf16[64,1,4,768]{3,2,1,0:T(4,128)(2,1)}), bf16[64,1,4,768]{3,2,1,0:T(4,128)(2,1)}, u32[]{:S(2)}, u32[]{:S(2)}) async-start(bf16[64,1,4,768]{3,2,1,0:T(4,128)(2,1)} %reshape.154), calls=%async_computation.3 | async-start | bytes 786432 | tf_op jit(solution)/shard_map/all_to_all | solution.py:33
  259.8 273.4 %all-reduce.2.cloned.1.call-start = ((), (), s32[]{:S(2)}) async-start(), calls=%async_computation.8 | async-start | bytes 1572864 | tf_op jit(solution)/shard_map/psum | solution.py:100
  260.1 4.9 copy-start.3
  260.1 4.9 copy-start.9
  265.0 4.0 copy-start.1
  269.3 10.6 %copy-start.6 = (f32[196,256]{1,0:T(8,128)}, f32[196,256]{1,0:T(8,128)S(1)}, u32[]{:S(2)}) copy-start(f32[196,256]{1,0:T(8,128)S(1)} %convolution_bitcast_fusion.1) | copy-start | bytes 602116
Sparse Core Ops, SparseCore 0:
  54.9 47.4 all-gather.4
  104.2 41.0 all-gather.2
  155.4 40.0 reduce-scatter.8
  198.0 48.5 reduce-scatter.10
  282.4 250.7 all-reduce.1
where the time goes:
time: 543 us; the launch traced here: 541 us
  waiting for transfers between devices  371 us (68%)
  blocking collectives  57.2 us (11%)
  local copies, waits for them, and re-layouts  37.9 us (7%)
  matrix products  29 us (5%)
  starting transfers between devices  23.4 us (4%)
  between operations  14 us (3%)
  other arithmetic  8.99 us (2%)
    psum x1, waiting for transfers between devices, per_device(): router_sum = lax.psum(router_term, ('expert', 'hidden'))  249 us
    unnamed x7, waiting for transfers between devices  71.7 us
    all_to_all x2, blocking collectives, to_experts(): lax.all_to_all(stacked_slots, 'expert', split_axis=2, concat_axis=0, tile...  57.2 us
    all_gather x2, waiting for transfers between devices, to_experts(): arrived = lax.all_gather(crossed, 'hidden', axis=0, tiled=True)  42.9 us
    all_to_all x2, starting transfers between devices, to_owners(): lax.all_to_all(summed, 'expert', split_axis=0, concat_axis=2, tiled=True)  22.6 us
    unnamed x29, local copies, waits for them, and re-layouts  15.3 us
  transfers between devices with their start and end apart: 7, of which 6 were waited for; matrix products, arithmetic and copies ran while one was open for 7% of the time, Pallas kernels for 0%

commit v1 on v0

v1 whole, which is shorter than its diff:
```python
import functools

import jax
import jax.numpy as jnp
from jax import lax
from jax.experimental import pallas as pl
from jax.experimental.pallas import tpu as pltpu
from jax.sharding import PartitionSpec as P

D = 768
SLOTS = 2
TOK = 196
PLANE = 32
RING = 8
ROWS = 128
COLS = 256
PIECES = 6
LANES = 6
MESH = pl.DeviceIdType.MESH
BF = jnp.bfloat16
F32 = jnp.float32


def place():
    expert = lax.axis_index("expert")
    h = lax.axis_index("hidden")
    p = (expert // 16) * 8 + expert % 8
    zhi = (expert // 8) % 2
    return p, zhi, h


def plane_device(q, zhi, h):
    return ((q // 8) * 16 + zhi * 8 + q % 8, h)


def ring_device(p, z):
    return ((p // 8) * 16 + (z // 4) * 8 + p % 8, z % 4)


def remote(src, dst, send, recv, device):
    return pltpu.make_async_remote_copy(
        src_ref=src, dst_ref=dst, send_sem=send, recv_sem=recv, device_id=device, device_id_type=MESH
    )


def greet(p, zhi, h, ring_offsets):
    barrier = pltpu.get_barrier_semaphore()
    z = zhi * 4 + h

    def one(j, carry):
        pl.semaphore_signal(
            barrier, inc=1, device_id=plane_device((p + j) % PLANE, zhi, h), device_id_type=MESH
        )
        return carry

    lax.fori_loop(1, PLANE, one, 0)
    for offset in ring_offsets:
        pl.semaphore_signal(
            barrier, inc=1, device_id=ring_device(p, (z + offset) % RING), device_id_type=MESH
        )
    pl.semaphore_wait(barrier, PLANE - 1 + len(ring_offsets))


def exchange_kernel(
    sa, sb, win, wout,
    out_a, out_b, gin, gout,
    prcv, fs, rows, tout, ttr, part, rr, ofin, otr, psend, prcv2,
    w_in, w_out, g_in, g_out, act, slope, dpre, acc,
    w_sem, g_sem, ps_send, ps_recv, po_send, po_recv,
    in_send, in_recv, t_send, t_recv, out_send, out_recv, ot_send, ot_recv,
):
    p, zhi, h = place()
    z = zhi * 4 + h
    near = {1: ring_device(p, (z + 1) % RING), -1: ring_device(p, (z + RING - 1) % RING)}
    lam = {1: h, -1: 3 - h}

    def pos(d, j):
        return j if d == 1 else 3 - j

    w_copies = [
        pltpu.make_async_copy(win, w_in, w_sem.at[0]),
        pltpu.make_async_copy(wout, w_out, w_sem.at[1]),
    ]
    for copy in w_copies:
        copy.start()
    greet(p, zhi, h, (1, RING - 1))

    sends = (sa, sb)

    def plane_copy(t, j):
        q = (p + j) % PLANE
        return remote(
            sends[t].at[q], prcv.at[t, p], ps_send.at[t, q], ps_recv.at[t, p], plane_device(q, zhi, h)
        )

    def plane_arrival(t, j):
        q = (p + j) % PLANE
        return remote(
            sends[t].at[q], prcv.at[t, q], ps_send.at[t, q], ps_recv.at[t, q], plane_device(q, zhi, h)
        )

    def loop(body):
        def step(j, carry):
            body(j)
            return carry

        lax.fori_loop(1, PLANE, step, 0)

    for t in (0, 1):
        loop(lambda j, t=t: plane_copy(t, j).start())

    def gather(t):
        prcv[t, p] = sends[t][p]
        loop(lambda j: plane_arrival(t, j).wait_recv())
        for c in range(LANES):
            lanes = slice(c * 128, (c + 1) * 128)
            fs[c] = prcv[t, :, :, lanes].astype(F32).reshape(COLS, 128)
            for s in range(4):
                piece = slice(s * PLANE, (s + 1) * PLANE)
                mine = fs[c, pl.ds(zhi * 4 + s, PLANE, stride=8), :]
                rows[t, z, piece, lanes] = mine.astype(BF)
                other = fs[c, pl.ds((1 - zhi) * 4 + s, PLANE, stride=8), :]
                tout[t, piece, lanes] = other.astype(BF)


    def in_item(d, i):
        own = lam[d] - i
        far = 3 - (i - lam[d] - 1)
        own_z = zhi * 4 + pos(d, own)
        far_z = (1 - zhi) * 4 + pos(d, far)
        return jnp.where(i <= lam[d], own_z, far_z)

    def rows_copy(t, d, zs, k):
        return remote(
            rows.at[t, zs], rows.at[t, zs], in_send.at[t, (1 - d) // 2, k], in_recv.at[t, zs], near[d]
        )

    def in_step(t, k, start):
        for d in (1, -1):
            i = k - jnp.where(lam[d] == 2, 1, 0)
            valid = jnp.logical_and(lam[d] <= 2, jnp.logical_and(i >= 0, i <= lam[d] + 2))

            @pl.when(valid)
            def _(d=d, i=i):
                zs = in_item(d, i)
                copy = rows_copy(t, d, zs, k)
                if start:

                    @pl.when(i > 0)
                    def _():
                        copy.wait_recv()

                    copy.start()
                else:
                    copy.wait_send()

            if k == 0:

                @pl.when(lam[d] == 2)
                def _(d=d):
                    copy = remote(tout.at[t], ttr.at[t], t_send.at[t, 0], t_recv.at[t], near[d])
                    copy.start() if start else copy.wait_send()

                @pl.when(lam[d] == 3)
                def _(d=d):
                    copy = remote(tout.at[t], rows.at[t, z], t_send.at[t, 0], in_recv.at[t, z], near[d])
                    copy.start() if start else copy.wait_send()

            if k == 1:

                @pl.when(lam[d] == 3)
                def _(d=d):
                    zs = zhi * 4 + pos(d, 2)
                    if start:
                        remote(tout.at[t], ttr.at[t], t_send.at[t, 0], t_recv.at[t], near[d]).wait_recv()
                    copy = remote(ttr.at[t], rows.at[t, zs], t_send.at[t, 1], in_recv.at[t, zs], near[d])
                    copy.start() if start else copy.wait_send()

    def in_last(t):
        for d in (1, -1):

            @pl.when(lam[d] == 3)
            def _(d=d):
                for own in (2, 1, 0):
                    rows_copy(t, d, zhi * 4 + pos(d, own), 0).wait_recv()
                for far in (3, 2):
                    rows_copy(t, d, (1 - zhi) * 4 + pos(d, far), 0).wait_recv()


    def out_step(t, k, start):
        for d in (1, -1):
            i = k - (3 - lam[d])
            valid = jnp.logical_and(i >= 0, i <= lam[d] + 1)

            @pl.when(valid)
            def _(d=d, i=i):
                far_z = (1 - zhi) * 4 + pos(d, 2 + i)
                own_z = zhi * 4 + pos(d, i - 2)
                zs = jnp.where(i <= 1, far_z, own_z)
                sem = out_send.at[t, (1 - d) // 2, k]
                if start:

                    @pl.when(lam[d] < 3)
                    def _():
                        remote(part.at[t, zs], rr.at[t, zs], sem, out_recv.at[t, zs], near[-d]).wait_recv()
                        part[t, zs] = (part[t, zs].astype(F32) + rr[t, zs].astype(F32)).astype(BF)

                @pl.when(lam[d] > 0)
                def _():
                    slot = zs
                    if d == -1:
                        slot = jnp.where(i - 2 == lam[d] - 1, RING, zs)
                    copy = remote(part.at[t, zs], rr.at[t, slot], sem, out_recv.at[t, slot], near[-d])
                    copy.start() if start else copy.wait_send()

                @pl.when(jnp.logical_and(lam[d] == 0, i == 0))
                def _():
                    copy = remote(part.at[t, zs], otr.at[t], sem, ot_recv.at[t, 0], near[-d])
                    copy.start() if start else copy.wait_send()

                @pl.when(jnp.logical_and(lam[d] == 0, i == 1))
                def _():
                    copy = remote(part.at[t, zs], ofin.at[t], sem, ot_recv.at[t, 1], near[-d])
                    copy.start() if start else copy.wait_send()

            if k == 5:

                @pl.when(lam[d] == 3)
                def _(d=d):
                    copy = remote(otr.at[t], ofin.at[t], ot_send.at[t], ot_recv.at[t, 1], near[-d])
                    if start:
                        remote(otr.at[t], otr.at[t], ot_send.at[t], ot_recv.at[t, 0], near[-d]).wait_recv()
                        copy.start()
                    else:
                        copy.wait_send()

    def out_last(t):
        @pl.when(h < 3)
        def _():
            remote(part.at[t, z], rr.at[t, z], ot_send.at[t], out_recv.at[t, z], near[1]).wait_recv()
            part[t, z] = (part[t, z].astype(F32) + rr[t, z].astype(F32)).astype(BF)

        @pl.when(h > 0)
        def _():
            remote(part.at[t, z], rr.at[t, RING], ot_send.at[t], out_recv.at[t, RING], near[1]).wait_recv()
            part[t, z] = (part[t, z].astype(F32) + rr[t, RING].astype(F32)).astype(BF)

        remote(otr.at[t], ofin.at[t], ot_send.at[t], ot_recv.at[t, 1], near[1]).wait_recv()
        for c in range(LANES):
            lanes = slice(c * 128, (c + 1) * 128)
            for s in range(4):
                piece = slice(s * PLANE, (s + 1) * PLANE)
                fs[c, pl.ds(zhi * 4 + s, PLANE, stride=8), :] = part[t, z, piece, lanes].astype(F32)
                fs[c, pl.ds((1 - zhi) * 4 + s, PLANE, stride=8), :] = ofin[t, piece, lanes].astype(F32)
            psend[t, :, :, lanes] = fs[c].reshape(PLANE, 8, 128).astype(BF)
        loop(lambda j: back_copy(t, j).start())
        prcv2[t, p] = psend[t, p]

    def back_copy(t, j):
        q = (p + j) % PLANE
        return remote(
            psend.at[t, q], prcv2.at[t, p], po_send.at[t, q], po_recv.at[t, p], plane_device(q, zhi, h)
        )

    def back_arrival(t, j):
        q = (p + j) % PLANE
        return remote(
            psend.at[t, q], prcv2.at[t, q], po_send.at[t, q], po_recv.at[t, q], plane_device(q, zhi, h)
        )


    def expert_rows(t, e):
        return rows[t, :, e * 64 : (e + 1) * 64, :].reshape(RING * 64, D)

    def forward_piece(k):
        e, f = k // 3, k % 3
        span = slice(f * COLS, (f + 1) * COLS)
        pre = jnp.dot(expert_rows(0, e), w_in[e, :, span], preferred_element_type=F32)
        half = 0.5 * (1.0 + lax.erf(pre * 0.7071067811865476))
        value = (pre * half).astype(BF)
        act[e, :, span] = value
        slope[e, :, span] = half + pre * jnp.exp(-0.5 * pre * pre) * 0.3989422804014327
        more = jnp.dot(value, w_out[e, span, :], preferred_element_type=F32)
        collect(0, e, f, more)

    def collect(t, e, f, more):
        if f == 0:
            acc[...] = more
        elif f == 1:
            acc[...] += more
        else:
            total = (acc[...] + more).astype(BF)
            part[t, :, e * 64 : (e + 1) * 64, :] = total.reshape(RING, 64, D)

    def backward_piece(k):
        e, f = k // 3, k % 3
        span = slice(f * COLS, (f + 1) * COLS)
        d_act = lax.dot_general(
            expert_rows(1, e), w_out[e, span, :], (((1,), (1,)), ((), ())), preferred_element_type=F32
        )
        value = (d_act * slope[e, :, span]).astype(BF)
        dpre[e, :, span] = value
        more = lax.dot_general(
            value, w_in[e, :, span], (((1,), (1,)), ((), ())), preferred_element_type=F32
        )
        collect(1, e, f, more)

    def weight_piece(k):
        e, f = k // 3, k % 3
        span = slice(f * COLS, (f + 1) * COLS)
        g_out[e, span, :] = lax.dot_general(
            act[e, :, span], expert_rows(1, e), (((0,), (0,)), ((), ())), preferred_element_type=F32
        ).astype(BF)
        g_in[e, :, span] = lax.dot_general(
            expert_rows(0, e), dpre[e, :, span], (((0,), (0,)), ((), ())), preferred_element_type=F32
        ).astype(BF)

    gather(0)
    in_step(0, 0, True)
    gather(1)
    for k in range(1, PIECES):
        in_step(0, k, True)
    in_last(0)
    for copy in w_copies:
        copy.wait()
    for k in range(PIECES):
        in_step(1, k, True)
        forward_piece(k)
    in_last(1)
    for k in range(PIECES):
        out_step(0, k, True)
        backward_piece(k)
    out_last(0)
    for k in range(PIECES):
        out_step(1, k, True)
        weight_piece(k)
    g_copies = [
        pltpu.make_async_copy(g_in, gin, g_sem.at[0]),
        pltpu.make_async_copy(g_out, gout, g_sem.at[1]),
    ]
    for copy in g_copies:
        copy.start()
    out_last(1)
    loop(lambda j: back_arrival(0, j).wait_recv())
    out_a[...] = prcv2[0]
    loop(lambda j: back_arrival(1, j).wait_recv())
    out_b[...] = prcv2[1]
    for t in (0, 1):
        loop(lambda j, t=t: plane_copy(t, j).wait_send())
        loop(lambda j, t=t: back_copy(t, j).wait_send())
        for k in range(PIECES):
            in_step(t, k, False)
            out_step(t, k, False)
    for copy in g_copies:
        copy.wait()


def exchange(send_a, send_b, weight_in, weight_out):
    vmem = pl.BlockSpec(memory_space=pltpu.VMEM)
    anywhere = pl.BlockSpec(memory_space=pl.ANY)
    dma = pltpu.SemaphoreType.DMA
    experts = weight_in.shape[0]
    width = weight_in.shape[2]
    return pl.pallas_call(
        exchange_kernel,
        out_shape=(
            jax.ShapeDtypeStruct(send_a.shape, BF),
            jax.ShapeDtypeStruct(send_a.shape, BF),
            jax.ShapeDtypeStruct(weight_in.shape, BF),
            jax.ShapeDtypeStruct(weight_out.shape, BF),
        ),
        in_specs=[vmem, vmem, anywhere, anywhere],
        out_specs=(vmem, vmem, anywhere, anywhere),
        scratch_shapes=[
            pltpu.VMEM((2, PLANE, 8, D), BF),
            pltpu.VMEM((LANES, COLS, 128), F32),
            pltpu.VMEM((2, RING, ROWS, D), BF),
            pltpu.VMEM((2, ROWS, D), BF),
            pltpu.VMEM((2, ROWS, D), BF),
            pltpu.VMEM((2, RING, ROWS, D), BF),
            pltpu.VMEM((2, RING + 1, ROWS, D), BF),
            pltpu.VMEM((2, ROWS, D), BF),
            pltpu.VMEM((2, ROWS, D), BF),
            pltpu.VMEM((2, PLANE, 8, D), BF),
            pltpu.VMEM((2, PLANE, 8, D), BF),
            pltpu.VMEM(weight_in.shape, BF),
            pltpu.VMEM(weight_out.shape, BF),
            pltpu.VMEM(weight_in.shape, BF),
            pltpu.VMEM(weight_out.shape, BF),
            pltpu.VMEM((experts, RING * 64, width), BF),
            pltpu.VMEM((experts, RING * 64, width), F32),
            pltpu.VMEM((experts, RING * 64, width), BF),
            pltpu.VMEM((RING * 64, D), F32),
            dma((2,)),
            dma((2,)),
            dma((2, PLANE)),
            dma((2, PLANE)),
            dma((2, PLANE)),
            dma((2, PLANE)),
            dma((2, 2, PIECES)),
            dma((2, RING)),
            dma((2, 2)),
            dma((2,)),
            dma((2, 2, PIECES)),
            dma((2, RING + 1)),
            dma((2,)),
            dma((2, 2)),
        ],
        compiler_params=pltpu.CompilerParams(
            collective_id=0, has_side_effects=True, vmem_limit_bytes=56 * 1024 * 1024
        ),
        name="exchange",
    )(send_a, send_b, weight_in, weight_out)


def window(h):
    return pl.multiple_of((h + h // 2) * 128, 128)


def router_kernel(rp, out, prcv, zs, zr, ps_send, ps_recv, z_send, z_recv):
    p, zhi, h = place()
    z = zhi * 4 + h
    greet(p, zhi, h, tuple(range(1, RING)))

    def loop(body):
        def step(j, carry):
            body(j)
            return carry

        lax.fori_loop(1, PLANE, step, 0)

    def plane_copy(j, slot):
        q = (p + j) % PLANE
        slot = p if slot is None else q
        return remote(rp.at[q], prcv.at[slot], ps_send.at[q], ps_recv.at[slot], plane_device(q, zhi, h))

    loop(lambda j: plane_copy(j, None).start())
    prcv[p] = rp[p]
    loop(lambda j: plane_copy(j, 1).wait_recv())
    zs[...] = jnp.sum(prcv[...].astype(F32), axis=0)
    zr[z] = zs[:, pl.ds(window(h), COLS)]

    def ring_copy(j, slot):
        to = (z + j) % RING
        slot = z if slot is None else to
        return remote(
            zs.at[:, pl.ds(window(to % 4), COLS)], zr.at[slot], z_send.at[to], z_recv.at[slot], ring_device(p, to)
        )

    for j in range(1, RING):
        ring_copy(j, None).start()
    for j in range(1, RING):
        ring_copy(j, 1).wait_recv()
    out[...] = jnp.sum(zr[...], axis=0)
    loop(lambda j: plane_copy(j, None).wait_send())
    for j in range(1, RING):
        ring_copy(j, None).wait_send()


def router_reduce(partial):
    vmem = pl.BlockSpec(memory_space=pltpu.VMEM)
    dma = pltpu.SemaphoreType.DMA
    return pl.pallas_call(
        router_kernel,
        out_shape=jax.ShapeDtypeStruct((8, COLS), F32),
        in_specs=[vmem],
        out_specs=vmem,
        scratch_shapes=[
            pltpu.VMEM((PLANE, 8, D), BF),
            pltpu.VMEM((8, D), F32),
            pltpu.VMEM((RING, 8, COLS), F32),
            dma((PLANE,)),
            dma((PLANE,)),
            dma((RING,)),
            dma((RING,)),
        ],
        compiler_params=pltpu.CompilerParams(collective_id=1, has_side_effects=True),
        name="router",
    )(partial)


def per_device(tokens, out_grad, slot_router, weight_in, weight_out):
    router = slot_router.reshape(D, 4, 2, 8, 4).transpose(0, 1, 3, 2, 4).reshape(D, COLS)
    logits = jnp.dot(tokens, router, preferred_element_type=F32)
    dispatch = jax.nn.softmax(logits, axis=0)
    combine = jax.nn.softmax(logits, axis=1)
    dispatch16 = dispatch.astype(BF)
    combine16 = combine.astype(BF)
    slot_in = jnp.einsum("tc,td->cd", dispatch16, tokens, preferred_element_type=F32).astype(BF)
    slot_grad = jnp.einsum("tc,td->cd", combine16, out_grad, preferred_element_type=F32).astype(BF)
    slot_out, slot_in_grad, grad_first, grad_second = exchange(
        slot_in.reshape(PLANE, 8, D), slot_grad.reshape(PLANE, 8, D), weight_in, weight_out
    )
    slot_out = slot_out.reshape(COLS, D)
    slot_in_grad = slot_in_grad.reshape(COLS, D)
    d_combine = jnp.einsum("td,cd->tc", out_grad, slot_out, preferred_element_type=F32)
    d_dispatch = jnp.einsum("td,cd->tc", tokens, slot_in_grad, preferred_element_type=F32)
    from_combine = combine * (d_combine - jnp.sum(combine * d_combine, axis=1, keepdims=True))
    from_dispatch = dispatch * (d_dispatch - jnp.sum(dispatch * d_dispatch, axis=0, keepdims=True))
    d_logits = (from_combine + from_dispatch).astype(BF)
    router_term = jnp.einsum("tc,td->cd", d_logits, tokens, preferred_element_type=F32).astype(BF)
    router_sum = router_reduce(router_term.reshape(PLANE, 8, D))
    token_grad = (
        jnp.dot(dispatch16, slot_in_grad, preferred_element_type=F32)
        + jnp.einsum("tc,dc->td", d_logits, router, preferred_element_type=F32)
    ).astype(BF)
    _, zhi, h = place()
    router_grad = lax.dynamic_slice(router_sum, (zhi * 4, (h % 2) * 64), (4, 192)).T
    return (token_grad, router_grad, grad_first, grad_second)


def solution(mesh):
    return jax.shard_map(
        per_device,
        mesh=mesh,
        in_specs=(
            P(("expert", "hidden"), None),
            P(("expert", "hidden"), None),
            P(),
            P("expert", None, "hidden"),
            P("expert", "hidden", None),
        ),
        out_specs=(
            P(("expert", "hidden"), None),
            P("hidden", "expert"),
            P("expert", None, "hidden"),
            P("expert", "hidden", None),
        ),
        check_vma=False,
    )
```

time: 543 us -> 183 us (0.34)
  waiting for transfers between devices: 371 us -> 0 us
  Pallas kernels: 0 us -> 167 us
  blocking collectives: 57.2 us -> 0 us
  local copies, waits for them, and re-layouts: 37.9 us -> 6.86 us
  starting transfers between devices: 23.4 us -> 0 us
  matrix products: 29 us -> 7.66 us
  between operations: 14 us -> 0.8 us
  other arithmetic: 8.99 us -> 0.36 us
    psum x1 -> x0, waiting for transfers between devices: 249 us -> none  [per_device(): router_sum = lax.psum(router_term, ('expert', 'hidden'))]
    pallas_call x0 -> x2, Pallas kernels: none -> 167 us  [the longest x1 148 us: exchange(): pl.pallas_call(exchange_kernel, out_shape=(jax.ShapeDtypeStruct(send_a.sh...]
    unnamed x7 -> x0, waiting for transfers between devices: 71.7 us -> none
    all_to_all x2 -> x0, blocking collectives: 57.2 us -> none  [to_experts(): lax.all_to_all(stacked_slots, 'expert', split_axis=2, concat_axis=0, tile...]
    all_gather x2 -> x0, waiting for transfers between devices: 42.9 us -> none  [to_experts(): arrived = lax.all_gather(crossed, 'hidden', axis=0, tiled=True)]
    all_to_all x2 -> x0, starting transfers between devices: 22.6 us -> none  [to_owners(): lax.all_to_all(summed, 'expert', split_axis=0, concat_axis=2, tiled=True)]
    dot_general x14 -> x8, matrix products: 29 us -> 7.66 us  [the longest x1 1.4 us: per_device(): jnp.einsum('td,cd->tc', out_grad, slot_out, preferred_element_type=F32)]
    unnamed x29 -> x13, local copies, waits for them, and re-layouts: 15.3 us -> 5.16 us
  transfers between devices with their start and end apart: 7 -> 0, of which waited for: 6 -> 0; matrix products, arithmetic and copies ran while one was open for 7% -> 0% of each run, Pallas kernels for 0% -> 0%
where the time goes in v1:
time: 183 us
  Pallas kernels  167 us (91%)
  matrix products  7.66 us (4%)
  local copies, waits for them, and re-layouts  6.86 us (4%)
    pallas_call x1, Pallas kernels, exchange(): pl.pallas_call(exchange_kernel, out_shape=(jax.ShapeDtypeStruct(send_a.sh...  148 us
    pallas_call x1, Pallas kernels, router_reduce(): pl.pallas_call(router_kernel, out_shape=jax.ShapeDtypeStruct((8, COLS), F...  18.5 us
    unnamed x13, local copies, waits for them, and re-layouts  5.16 us

profile of v1, /device:TPU:1, one launch (start us, length us, event | category | flops | bytes accessed | tf_op | source)
XLA Modules:
  0.0 182.5 jit_solution(18385281730964822916)
XLA Ops:
  0.6 0.0 copy-start
  0.6 0.0 copy-start.4
  0.7 1.2 copy.9
  1.9 0.1 reshape.35
  2.0 0.1 copy.10
  2.2 0.1 reshape.36
  2.3 0.0 copy-done
  2.3 0.4 fusion.18
  2.7 0.2 fusion.11
  2.9 0.0 copy-done.4
  2.9 1.2 fusion.2.sb
  4.1 1.1 fusion.1.sa
  5.1 148.3 %exchange.1 = (bf16[32,8,768]{2,1,0:T(8,128)(2,1)}, bf16[32,8,768]{2,1,0:T(8,128)(2,1)}, bf16[2,768,768]{2,1,0:T(8,128)(2,1)}, bf16[2,768,768]{2,1,0:T(8,128)(2,1)}) custom-call(bf16[32,8,768]{2,1,0:T(8,128)(2,1)} %fusion.1.sa, bf16[32,8,768]{2,1,0:T(8,128)(2,1)} %fusion.2.sb, bf16[2,768,768]{2,1,0:T(8,128)(2,1)} %win.1, bf16[2,768,768]{2,1,0:T(8,128)(2,1)} %wout.1), custom_call_target="tpu_custom_call" | custom-call | tf_op jit(solution)/shard_map/exchange/pallas_call | solution.py:364
  153.4 0.0 copy-start.3
  153.5 1.4 convolution_bitcast_fusion
  154.8 1.4 multiply_reduce_fusion.1
  156.2 0.0 copy-start.2
  156.2 0.2 add_convert_fusion
  156.4 0.0 copy-done.3
  156.4 0.2 fusion.6
  156.7 1.0 fusion
  157.6 1.0 fusion.3.rp
  158.7 18.5 %router.1 = f32[8,256]{1,0:T(8,128)} custom-call(bf16[32,8,768]{2,1,0:T(8,128)(2,1)} %fusion.3.rp), custom_call_target="tpu_custom_call" | custom-call | tf_op jit(solution)/shard_map/router/pallas_call | solution.py:463
  177.2 1.4 dynamic-slice_bitcast_fusion
  178.6 0.0 copy-done.2
  178.6 0.0 copy-start.1
  178.6 1.4 copy.13
  180.0 1.1 copy-done.1
  181.1 1.4 copy.14
Async XLA Ops:
  0.6 1.6 copy-start
  0.6 2.2 %copy-start.4 = (bf16[196,768]{1,0:T(8,128)(2,1)S(1)}, bf16[196,768]{1,0:T(8,128)(2,1)}, u32[]{:S(2)}) copy-start(bf16[196,768]{1,0:T(8,128)(2,1)} %param.6) | copy-start | bytes 903172
  153.4 2.9 %copy-start.3 = (bf16[32,8,768]{2,1,0:T(8,128)(2,1)S(1)}, bf16[32,8,768]{2,1,0:T(8,128)(2,1)}, u32[]{:S(2)}) copy-start(bf16[32,8,768]{2,1,0:T(8,128)(2,1)} %get-tuple-element.8) | copy-start | bytes 1179652
  156.2 22.4 %copy-start.2 = (bf16[2,768,768]{2,1,0:T(8,128)(2,1)S(1)}, bf16[2,768,768]{2,1,0:T(8,128)(2,1)}, u32[]{:S(2)}) copy-start(bf16[2,768,768]{2,1,0:T(8,128)(2,1)} %get-tuple-element.26) | copy-start | bytes 7077892
  178.6 2.5 %copy-start.1 = (bf16[2,768,768]{2,1,0:T(8,128)(2,1)S(1)}, bf16[2,768,768]{2,1,0:T(8,128)(2,1)}, u32[]{:S(2)}) copy-start(bf16[2,768,768]{2,1,0:T(8,128)(2,1)} %get-tuple-element.27) | copy-start | bytes 7077892

commit v2 on v1

v2 whole, which is shorter than its diff:
```python
import functools

import jax
import jax.numpy as jnp
from jax import lax
from jax.experimental import pallas as pl
from jax.experimental.pallas import tpu as pltpu
from jax.sharding import PartitionSpec as P

D = 768
SLOTS = 2
TOK = 196
PLANE = 32
RING = 8
ROWS = 128
COLS = 256
HALF = 64
COPIES = 80
LANES = 6
MESH = pl.DeviceIdType.MESH
BF = jnp.bfloat16
F32 = jnp.float32


def place():
    expert = lax.axis_index("expert")
    h = lax.axis_index("hidden")
    p = lax.div(expert, 16) * 8 + lax.rem(expert, 8)
    zhi = lax.rem(lax.div(expert, 8), 2)
    return p, zhi, h


def plane_device(q, zhi, h):
    return (lax.div(q, 8) * 16 + zhi * 8 + lax.rem(q, 8), h)


def ring_device(p, z):
    return (lax.div(p, 8) * 16 + lax.div(z, 4) * 8 + lax.rem(p, 8), lax.rem(z, 4))


def remote(src, dst, send, recv, device):
    return pltpu.make_async_remote_copy(
        src_ref=src, dst_ref=dst, send_sem=send, recv_sem=recv, device_id=device, device_id_type=MESH
    )


def greet(p, zhi, h, ring_offsets):
    barrier = pltpu.get_barrier_semaphore()
    z = zhi * 4 + h

    def one(j, carry):
        pl.semaphore_signal(
            barrier, inc=1, device_id=plane_device(lax.rem(p + j, PLANE), zhi, h), device_id_type=MESH
        )
        return carry

    lax.fori_loop(1, PLANE, one, 0)
    for offset in ring_offsets:
        pl.semaphore_signal(
            barrier, inc=1, device_id=ring_device(p, (z + offset) % RING), device_id_type=MESH
        )
    pl.semaphore_wait(barrier, PLANE - 1 + len(ring_offsets))


EVENTS = (
    ("gather",),
    ("fwd", 0),
    ("fwd", 1),
    ("bwd", 0),
    ("wg", 0, 0),
    ("wg", 0, 1),
    ("wg", 0, 2),
    ("bwd", 1),
    ("wg", 1, 0),
    ("wg", 1, 1),
    ("wg", 1, 2),
    ("last", 0),
    ("last", 1),
)
EDGE = (
    (("io", 0, "l", 0), ("iO", 0, "h", 3), ("io", 1, "l", 0), ("iO", 1, "h", 3)),
    (("iX", 0, "l", 3), ("ix", 0, "h", 2), ("iX", 1, "l", 3), ("iO", 2, "h", 3), ("iX", 0, "l", 2), ("iO", 3, "h", 3), ("ix", 1, "h", 2), ("iX", 2, "l", 3), ("io", 2, "l", 0), ("iX", 1, "l", 2), ("iX", 3, "l", 3), ("io", 3, "l", 0)),
    (("oX", 0, "h", 2), ("oX", 0, "h", 3), ("oo", 0, "h", 0)),
    (("oo", 0, "h", 1), ("ix", 2, "h", 2), ("oo", 0, "h", 2), ("oX", 1, "h", 2), ("iX", 2, "l", 2), ("oX", 1, "h", 3), ("oo", 1, "h", 0), ("ix", 3, "h", 2), ("oo", 1, "h", 1), ("oo", 1, "h", 2), ("oX", 0, "l", 2), ("iX", 3, "l", 2), ("oX", 0, "l", 3), ("oT", 0, "h", 2)),
    (("oX", 2, "h", 2),),
    (("oX", 2, "h", 3),),
    (("oo", 2, "h", 0),),
    (("oo", 2, "h", 1),),
    (("oo", 2, "h", 2),),
    (("oX", 3, "h", 2), ("oX", 1, "l", 2)),
    (("oX", 3, "h", 3), ("oX", 1, "l", 3)),
    (("oT", 1, "h", 2), ("oo", 3, "h", 0)),
    (("oX", 2, "l", 2), ("oo", 3, "h", 1), ("oX", 2, "l", 3), ("oT", 2, "h", 2), ("oo", 3, "h", 2), ("oX", 3, "l", 2), ("oX", 3, "l", 3), ("oT", 3, "h", 2)),
    (),
)
INNER = (
    (("io", 0, "l", 1), ("iy", 0, "h", 2), ("io", 0, "h", 2), ("io", 1, "l", 1)),
    (("io", 0, "h", 1), ("io", 0, "l", 0), ("io", 1, "l", 0), ("iy", 1, "h", 2), ("io", 0, "h", 0), ("iX", 0, "l", 3), ("io", 1, "h", 0), ("iX", 1, "l", 3), ("iX", 0, "h", 3), ("iX", 0, "l", 2), ("iX", 1, "h", 3), ("iX", 2, "l", 3)),
    (("iX", 0, "h", 2), ("io", 2, "l", 0), ("io", 1, "h", 1), ("iX", 1, "l", 2), ("io", 1, "h", 2), ("io", 2, "l", 1)),
    (("iX", 1, "h", 2), ("iX", 3, "l", 3), ("iy", 2, "h", 2), ("io", 3, "l", 0), ("oX", 0, "h", 2), ("iX", 2, "h", 3), ("oX", 0, "h", 3), ("io", 2, "h", 0), ("io", 2, "h", 1), ("io", 3, "l", 1), ("oo", 0, "h", 0), ("io", 2, "h", 2), ("oo", 0, "h", 1), ("iy", 3, "h", 2), ("oX", 1, "h", 2), ("iX", 3, "h", 3), ("oX", 0, "l", 2), ("iX", 2, "l", 2), ("oX", 0, "l", 3), ("oX", 1, "h", 3)),
    (("oo", 1, "h", 0), ("iX", 2, "h", 2), ("oo", 1, "h", 1), ("io", 3, "h", 0)),
    (("io", 3, "h", 1), ("iX", 3, "l", 2)),
    (("io", 3, "h", 2),),
    (),
    (("iX", 3, "h", 2), ("oX", 2, "h", 2), ("oo", 0, "l", 0), ("oX", 2, "h", 3)),
    (("oX", 1, "l", 2),),
    (("oo", 2, "h", 0), ("oX", 1, "l", 3)),
    (("oo", 2, "h", 1), ("oo", 1, "l", 0), ("oX", 2, "l", 2), ("oX", 3, "h", 2), ("oX", 2, "l", 3), ("oX", 3, "h", 3), ("oo", 2, "l", 0)),
    (("oX", 3, "l", 2), ("oo", 3, "h", 0), ("oX", 3, "l", 3), ("oo", 3, "h", 1), ("oo", 3, "l", 0)),
    (),
)

class Chains:
    def __init__(self, edge, at, refs):
        self.lam = {"h": 3, "l": 0} if edge else {"h": 2, "l": 1}
        self.at = at
        self.refs = refs
        self.sent = 0
        self.seen = set()

    def zpos(self, d, j, own):
        up, zhi = self.at["up"], self.at["zhi"]
        towards = up if d == "h" else 1 - up
        return (zhi if own else 1 - zhi) * 4 + jnp.where(towards == 1, j, 3 - j)

    def last_slot(self, d):
        towards = self.at["up"] if d == "h" else 1 - self.at["up"]
        return jnp.where(towards == 1, self.at["z"], RING)

    def block(self, name, q, slot=None):
        t, e = q // 2, q % 2
        rows = pl.ds(e * HALF, HALF)
        ref = self.refs[name]
        return ref.at[t, rows] if slot is None else ref.at[t, slot, rows]

    def copy(self, src, dst, recv, device):
        remote(src, dst, self.refs["z_send"].at[self.sent], recv, device).start()
        self.sent += 1

    def drain(self):
        for n in range(self.sent):
            one = self.block("tout", 0)
            remote(one, one, self.refs["z_send"].at[n], self.refs["t_recv"].at[0], self.at["h"]).wait_send()

    def arrive(self, dst, recv):
        remote(dst, dst, self.refs["z_send"].at[0], recv, self.at["h"]).wait_recv()

    def arrive_rows(self, q, d, j, own):
        if (q, d, j, own) in self.seen:
            return
        self.seen.add((q, d, j, own))
        zs = self.zpos(d, j, own)
        self.arrive(self.block("rows", q, zs), self.refs["in_recv"].at[q, zs])

    def all_rows(self, q):
        for d in ("h", "l"):
            for j in range(self.lam[d] - 1, -1, -1):
                self.arrive_rows(q, d, j, True)
            for j in (3, 2):
                self.arrive_rows(q, d, j, False)

    def add(self, q, zs, slot):
        self.arrive(self.block("rr", q, slot), self.refs["out_recv"].at[q, slot])
        part, rr = self.block("part", q, zs), self.block("rr", q, slot)
        part[...] = (part[...].astype(F32) + rr[...].astype(F32)).astype(BF)

    def finish(self, q):
        for d in ("h", "l"):
            if self.lam[d] < 3:
                self.add(q, self.at["z"], self.last_slot(d))
        self.arrive(self.block("ofin", q), self.refs["ot_recv"].at[q, 1])

    def emit(self, code, q, d, j):
        lam = self.lam[d]
        other = "l" if d == "h" else "h"
        in_recv, out_recv = self.refs["in_recv"], self.refs["out_recv"]
        if code in ("io", "iX"):
            own = code == "io"
            zs = self.zpos(d, j, own)
            if not own or j < lam:
                self.arrive_rows(q, d, j, own)
            rows = self.block("rows", q, zs)
            self.copy(rows, rows, in_recv.at[q, zs], self.at[d])
        elif code == "iO":
            z = self.at["z"]
            self.copy(self.block("tout", q), self.block("rows", q, z), in_recv.at[q, z], self.at[d])
        elif code == "iy":
            self.copy(self.block("tout", q), self.block("ttr", q), self.refs["t_recv"].at[q], self.at[d])
        elif code == "ix":
            ttr = self.block("ttr", q)
            self.arrive(ttr, self.refs["t_recv"].at[q])
            zs = self.zpos(d, 2, True)
            self.copy(ttr, self.block("rows", q, zs), in_recv.at[q, zs], self.at[d])
        elif code in ("oo", "oX"):
            own = code == "oo"
            zs = self.zpos(d, j, own)
            if lam < 3:
                self.add(q, zs, zs)
            part = self.block("part", q, zs)
            if lam > 0:
                slot = self.last_slot_of(d, zs) if own and j == lam - 1 else zs
                self.copy(part, self.block("rr", q, slot), out_recv.at[q, slot], self.at[other])
            elif j == 2:
                self.copy(part, self.block("otr", q), self.refs["ot_recv"].at[q, 0], self.at[other])
            else:
                self.copy(part, self.block("ofin", q), self.refs["ot_recv"].at[q, 1], self.at[other])
        else:
            otr = self.block("otr", q)
            self.arrive(otr, self.refs["ot_recv"].at[q, 0])
            self.copy(otr, self.block("ofin", q), self.refs["ot_recv"].at[q, 1], self.at[other])

    def last_slot_of(self, d, zs):
        towards = self.at["up"] if d == "h" else 1 - self.at["up"]
        return jnp.where(towards == 1, zs, RING)


def exchange_kernel(
    sa, sb, win, wout,
    out_a, out_b, gin, gout,
    prcv, fs, rows, tout, ttr, part, rr, ofin, otr, psend, prcv2,
    w_in, w_out, g_in, g_out, act, slope, dpre, acc,
    w_sem, g_sem, ps_send, ps_recv, po_send, po_recv,
    z_send, in_recv, t_recv, out_recv, ot_recv,
):
    p, zhi, h = place()
    z = zhi * 4 + h
    up = jnp.where(h >= 2, 1, 0)
    step = 2 * up - 1
    at = {
        "z": z,
        "zhi": zhi,
        "up": up,
        "h": ring_device(p, (z + step + RING) % RING),
        "l": ring_device(p, (z - step + RING) % RING),
    }
    refs = {
        "rows": rows, "tout": tout, "ttr": ttr, "part": part, "rr": rr, "ofin": ofin, "otr": otr,
        "z_send": z_send, "in_recv": in_recv, "t_recv": t_recv, "out_recv": out_recv, "ot_recv": ot_recv,
    }
    edge, inner = Chains(True, at, refs), Chains(False, at, refs)
    at_edge = jnp.logical_or(h == 0, h == 3)

    def both(body):
        @pl.when(at_edge)
        def _():
            body(edge, EDGE)

        @pl.when(jnp.logical_not(at_edge))
        def _():
            body(inner, INNER)

    w_copies = [
        pltpu.make_async_copy(win, w_in, w_sem.at[0]),
        pltpu.make_async_copy(wout, w_out, w_sem.at[1]),
    ]
    for copy in w_copies:
        copy.start()
    greet(p, zhi, h, (1, RING - 1))
    sends = (sa, sb)
    for t in (0, 1):
        plane_start(p, zhi, h, sends[t], prcv.at[t], ps_send.at[t], ps_recv.at[t])

    def gather(t):
        plane_arrived(prcv.at[t], ps_recv.at[t])
        prcv[t, p] = sends[t][p]
        for c in range(LANES):
            lanes = slice(c * 128, (c + 1) * 128)
            fs[c] = prcv[t, :, :, lanes].astype(F32).reshape(COLS, 128)
            for s in range(4):
                piece = slice(s * PLANE, (s + 1) * PLANE)
                mine = fs[c, pl.ds(zhi * 4 + s, PLANE, stride=8), :]
                rows[t, z, piece, lanes] = mine.astype(BF)
                other = fs[c, pl.ds((1 - zhi) * 4 + s, PLANE, stride=8), :]
                tout[t, piece, lanes] = other.astype(BF)

    def out_last(t):
        def finish(chains, table):
            for e in (0, 1):
                chains.finish(2 * t + e)

        both(finish)
        for c in range(LANES):
            lanes = slice(c * 128, (c + 1) * 128)
            for s in range(4):
                piece = slice(s * PLANE, (s + 1) * PLANE)
                fs[c, pl.ds(zhi * 4 + s, PLANE, stride=8), :] = part[t, z, piece, lanes].astype(F32)
                fs[c, pl.ds((1 - zhi) * 4 + s, PLANE, stride=8), :] = ofin[t, piece, lanes].astype(F32)
            psend[t, :, :, lanes] = fs[c].reshape(PLANE, 8, 128).astype(BF)
        plane_start(p, zhi, h, psend.at[t], prcv2.at[t], po_send.at[t], po_recv.at[t])


    def expert_rows(t, e):
        return rows[t, :, e * HALF : (e + 1) * HALF, :].reshape(RING * HALF, D)

    def collect(t, e, f, more):
        if f == 0:
            acc[...] = more
        elif f == 1:
            acc[...] += more
        else:
            total = (acc[...] + more).astype(BF)
            part[t, :, e * HALF : (e + 1) * HALF, :] = total.reshape(RING, HALF, D)

    def forward_piece(e, f):
        span = slice(f * COLS, (f + 1) * COLS)
        pre = jnp.dot(expert_rows(0, e), w_in[e, :, span], preferred_element_type=F32)
        half = 0.5 * (1.0 + lax.erf(pre * 0.7071067811865476))
        value = (pre * half).astype(BF)
        act[e, :, span] = value
        slope[e, :, span] = half + pre * jnp.exp(-0.5 * pre * pre) * 0.3989422804014327
        more = jnp.dot(value, w_out[e, span, :], preferred_element_type=F32)
        collect(0, e, f, more)

    def backward_piece(e, f):
        span = slice(f * COLS, (f + 1) * COLS)
        d_act = lax.dot_general(
            expert_rows(1, e), w_out[e, span, :], (((1,), (1,)), ((), ())), preferred_element_type=F32
        )
        value = (d_act * slope[e, :, span]).astype(BF)
        dpre[e, :, span] = value
        more = lax.dot_general(
            value, w_in[e, :, span], (((1,), (1,)), ((), ())), preferred_element_type=F32
        )
        collect(1, e, f, more)

    def weight_piece(e, f):
        span = slice(f * COLS, (f + 1) * COLS)
        g_out[e, span, :] = lax.dot_general(
            act[e, :, span], expert_rows(1, e), (((0,), (0,)), ((), ())), preferred_element_type=F32
        ).astype(BF)
        g_in[e, :, span] = lax.dot_general(
            expert_rows(0, e), dpre[e, :, span], (((0,), (0,)), ((), ())), preferred_element_type=F32
        ).astype(BF)

    g_copies = [
        pltpu.make_async_copy(g_in, gin, g_sem.at[0]),
        pltpu.make_async_copy(g_out, gout, g_sem.at[1]),
    ]

    def segment(n):
        def body(chains, table):
            for item in table[n]:
                chains.emit(*item)

        both(body)

    gather(0)
    for n, event in enumerate(EVENTS):
        segment(n)
        kind, which = event[0], event[1:]
        if kind == "gather":
            gather(1)
        elif kind in ("fwd", "bwd"):
            (e,) = which
            q = e if kind == "fwd" else 2 + e
            both(lambda chains, table, q=q: chains.all_rows(q))
            if q == 0:
                for copy in w_copies:
                    copy.wait()
            for f in range(3):
                (forward_piece if kind == "fwd" else backward_piece)(e, f)
        elif kind == "wg":
            weight_piece(*which)
            if which == (1, 2):
                for copy in g_copies:
                    copy.start()
        else:
            out_last(which[0])
    segment(len(EVENTS))
    plane_arrived(prcv2.at[0], po_recv.at[0])
    prcv2[0, p] = psend[0, p]
    out_a[...] = prcv2[0]
    plane_arrived(prcv2.at[1], po_recv.at[1])
    prcv2[1, p] = psend[1, p]
    out_b[...] = prcv2[1]
    for t in (0, 1):
        plane_sent(prcv.at[t], ps_send.at[t])
        plane_sent(psend.at[t], po_send.at[t])

    both(lambda chains, table: chains.drain())
    for copy in g_copies:
        copy.wait()


def plane_start(p, zhi, h, src, dst, send, recv):
    def step(j, carry):
        q = lax.rem(p + j, PLANE)
        remote(src.at[q], dst.at[p], send, recv, plane_device(q, zhi, h)).start()
        return carry

    lax.fori_loop(1, PLANE, step, 0)


def plane_arrived(dst, recv):
    many = dst.at[pl.ds(0, PLANE - 1)]
    pltpu.make_async_copy(many, many, recv).wait()


def plane_sent(src, send):
    many = src.at[pl.ds(0, PLANE - 1)]
    pltpu.make_async_copy(many, many, send).wait()


def exchange(send_a, send_b, weight_in, weight_out):
    vmem = pl.BlockSpec(memory_space=pltpu.VMEM)
    anywhere = pl.BlockSpec(memory_space=pl.ANY)
    dma = pltpu.SemaphoreType.DMA
    experts = weight_in.shape[0]
    width = weight_in.shape[2]
    return pl.pallas_call(
        exchange_kernel,
        out_shape=(
            jax.ShapeDtypeStruct(send_a.shape, BF),
            jax.ShapeDtypeStruct(send_a.shape, BF),
            jax.ShapeDtypeStruct(weight_in.shape, BF),
            jax.ShapeDtypeStruct(weight_out.shape, BF),
        ),
        in_specs=[vmem, vmem, anywhere, anywhere],
        out_specs=(vmem, vmem, anywhere, anywhere),
        scratch_shapes=[
            pltpu.VMEM((2, PLANE, 8, D), BF),
            pltpu.VMEM((LANES, COLS, 128), F32),
            pltpu.VMEM((2, RING, ROWS, D), BF),
            pltpu.VMEM((2, ROWS, D), BF),
            pltpu.VMEM((2, ROWS, D), BF),
            pltpu.VMEM((2, RING, ROWS, D), BF),
            pltpu.VMEM((2, RING + 1, ROWS, D), BF),
            pltpu.VMEM((2, ROWS, D), BF),
            pltpu.VMEM((2, ROWS, D), BF),
            pltpu.VMEM((2, PLANE, 8, D), BF),
            pltpu.VMEM((2, PLANE, 8, D), BF),
            pltpu.VMEM(weight_in.shape, BF),
            pltpu.VMEM(weight_out.shape, BF),
            pltpu.VMEM(weight_in.shape, BF),
            pltpu.VMEM(weight_out.shape, BF),
            pltpu.VMEM((experts, RING * 64, width), BF),
            pltpu.VMEM((experts, RING * 64, width), F32),
            pltpu.VMEM((experts, RING * 64, width), BF),
            pltpu.VMEM((RING * 64, D), F32),
            dma((2,)),
            dma((2,)),
            dma((2,)),
            dma((2,)),
            dma((2,)),
            dma((2,)),
            dma((COPIES,)),
            dma((4, RING)),
            dma((4,)),
            dma((4, RING + 1)),
            dma((4, 2)),
        ],
        compiler_params=pltpu.CompilerParams(
            collective_id=0, has_side_effects=True, vmem_limit_bytes=56 * 1024 * 1024
        ),
        name="exchange",
    )(send_a, send_b, weight_in, weight_out)


def window(h):
    return pl.multiple_of((h + h // 2) * 128, 128)


def router_kernel(rp, out, prcv, zs, zr, ps_send, ps_recv, z_send, z_recv):
    p, zhi, h = place()
    z = zhi * 4 + h
    greet(p, zhi, h, tuple(range(1, RING)))

    plane_start(p, zhi, h, rp, prcv, ps_send, ps_recv)
    plane_arrived(prcv, ps_recv)
    prcv[p] = rp[p]
    zs[...] = jnp.sum(prcv[...].astype(F32), axis=0)
    zr[z] = zs[:, pl.ds(window(h), COLS)]

    def ring_copy(j, slot):
        to = lax.rem(z + j, RING)
        slot = z if slot is None else to
        return remote(
            zs.at[:, pl.ds(window(lax.rem(to, 4)), COLS)],
            zr.at[slot],
            z_send.at[to],
            z_recv.at[slot],
            ring_device(p, to),
        )

    for j in range(1, RING):
        ring_copy(j, None).start()
    for j in range(1, RING):
        ring_copy(j, 1).wait_recv()
    out[...] = jnp.sum(zr[...], axis=0)
    plane_sent(rp, ps_send)
    for j in range(1, RING):
        ring_copy(j, None).wait_send()


def router_reduce(partial):
    vmem = pl.BlockSpec(memory_space=pltpu.VMEM)
    dma = pltpu.SemaphoreType.DMA
    return pl.pallas_call(
        router_kernel,
        out_shape=jax.ShapeDtypeStruct((8, COLS), F32),
        in_specs=[vmem],
        out_specs=vmem,
        scratch_shapes=[
            pltpu.VMEM((PLANE, 8, D), BF),
            pltpu.VMEM((8, D), F32),
            pltpu.VMEM((RING, 8, COLS), F32),
            dma(()),
            dma(()),
            dma((RING,)),
            dma((RING,)),
        ],
        compiler_params=pltpu.CompilerParams(collective_id=1, has_side_effects=True),
        name="router",
    )(partial)


def per_device(tokens, out_grad, slot_router, weight_in, weight_out):
    router = slot_router.reshape(D, 4, 2, 8, 4).transpose(0, 1, 3, 2, 4).reshape(D, COLS)
    logits = jnp.dot(tokens, router, preferred_element_type=F32)
    dispatch = jax.nn.softmax(logits, axis=0)
    combine = jax.nn.softmax(logits, axis=1)
    dispatch16 = dispatch.astype(BF)
    combine16 = combine.astype(BF)
    slot_in = jnp.einsum("tc,td->cd", dispatch16, tokens, preferred_element_type=F32).astype(BF)
    slot_grad = jnp.einsum("tc,td->cd", combine16, out_grad, preferred_element_type=F32).astype(BF)
    slot_out, slot_in_grad, grad_first, grad_second = exchange(
        slot_in.reshape(PLANE, 8, D), slot_grad.reshape(PLANE, 8, D), weight_in, weight_out
    )
    slot_out = slot_out.reshape(COLS, D)
    slot_in_grad = slot_in_grad.reshape(COLS, D)
    d_combine = jnp.einsum("td,cd->tc", out_grad, slot_out, preferred_element_type=F32)
    d_dispatch = jnp.einsum("td,cd->tc", tokens, slot_in_grad, preferred_element_type=F32)
    from_combine = combine * (d_combine - jnp.sum(combine * d_combine, axis=1, keepdims=True))
    from_dispatch = dispatch * (d_dispatch - jnp.sum(dispatch * d_dispatch, axis=0, keepdims=True))
    d_logits = (from_combine + from_dispatch).astype(BF)
    router_term = jnp.einsum("tc,td->cd", d_logits, tokens, preferred_element_type=F32).astype(BF)
    router_sum = router_reduce(router_term.reshape(PLANE, 8, D))
    token_grad = (
        jnp.dot(dispatch16, slot_in_grad, preferred_element_type=F32)
        + jnp.einsum("tc,dc->td", d_logits, router, preferred_element_type=F32)
    ).astype(BF)
    _, zhi, h = place()
    router_grad = lax.dynamic_slice(router_sum, (zhi * 4, (h % 2) * 64), (4, 192)).T
    return (token_grad, router_grad, grad_first, grad_second)


def solution(mesh):
    return jax.shard_map(
        per_device,
        mesh=mesh,
        in_specs=(
            P(("expert", "hidden"), None),
            P(("expert", "hidden"), None),
            P(),
            P("expert", None, "hidden"),
            P("expert", "hidden", None),
        ),
        out_specs=(
            P(("expert", "hidden"), None),
            P("hidden", "expert"),
            P("expert", None, "hidden"),
            P("expert", "hidden", None),
        ),
        check_vma=False,
    )
```

time: 183 us -> 151 us (0.83)
  Pallas kernels: 167 us -> 135 us
    pallas_call x1, Pallas kernels: 148 us -> 115 us  [exchange(): pl.pallas_call(exchange_kernel, out_shape=(jax.ShapeDtypeStruct(send_a.sh...]
    pallas_call x1, Pallas kernels: 18.5 us -> 20.5 us  [router_reduce(): pl.pallas_call(router_kernel, out_shape=jax.ShapeDtypeStruct((8, COLS), F...]
where the time goes in v2:
time: 151 us
  Pallas kernels  135 us (89%)
  matrix products  7.65 us (5%)
  local copies, waits for them, and re-layouts  6.86 us (5%)
    pallas_call x1, Pallas kernels, exchange(): pl.pallas_call(exchange_kernel, out_shape=(jax.ShapeDtypeStruct(send_a.sh...  115 us
    pallas_call x1, Pallas kernels, router_reduce(): pl.pallas_call(router_kernel, out_shape=jax.ShapeDtypeStruct((8, COLS), F...  20.5 us
    unnamed x13, local copies, waits for them, and re-layouts  5.16 us

profile of v2, /device:TPU:1, one launch (start us, length us, event | category | flops | bytes accessed | tf_op | source)
XLA Modules:
  0.0 150.7 jit_solution(2097508432538525951)
XLA Ops:
  0.6 0.0 copy-start
  0.6 0.0 copy-start.4
  0.7 1.2 copy.9
  1.9 0.1 reshape.35
  2.0 0.1 copy.10
  2.2 0.1 reshape.36
  2.3 0.0 copy-done
  2.3 0.4 fusion.18
  2.7 0.2 fusion.11
  2.9 0.0 copy-done.4
  2.9 1.2 fusion.2.sb
  4.0 1.1 fusion.1.sa
  5.1 114.5 %exchange.1 = (bf16[32,8,768]{2,1,0:T(8,128)(2,1)}, bf16[32,8,768]{2,1,0:T(8,128)(2,1)}, bf16[2,768,768]{2,1,0:T(8,128)(2,1)}, bf16[2,768,768]{2,1,0:T(8,128)(2,1)}) custom-call(bf16[32,8,768]{2,1,0:T(8,128)(2,1)} %fusion.1.sa, bf16[32,8,768]{2,1,0:T(8,128)(2,1)} %fusion.2.sb, bf16[2,768,768]{2,1,0:T(8,128)(2,1)} %win.1, bf16[2,768,768]{2,1,0:T(8,128)(2,1)} %wout.1), custom_call_target="tpu_custom_call" | custom-call | tf_op jit(solution)/shard_map/exchange/pallas_call | solution.py:410
  119.7 0.0 copy-start.3
  119.7 1.4 convolution_bitcast_fusion
  121.0 1.4 multiply_reduce_fusion.1
  122.4 0.0 copy-start.2
  122.4 0.2 add_convert_fusion
  122.6 0.0 copy-done.3
  122.6 0.3 fusion.6
  122.9 1.0 fusion
  123.8 1.0 fusion.3.rp
  124.9 20.5 %router.1 = f32[8,256]{1,0:T(8,128)} custom-call(bf16[32,8,768]{2,1,0:T(8,128)(2,1)} %fusion.3.rp), custom_call_target="tpu_custom_call" | custom-call | tf_op jit(solution)/shard_map/router/pallas_call | solution.py:498
  145.4 1.4 dynamic-slice_bitcast_fusion
  146.7 0.0 copy-done.2
  146.7 0.0 copy-start.1
  146.7 1.4 copy.13
  148.1 1.1 copy-done.1
  149.2 1.4 copy.14
Async XLA Ops:
  0.6 1.6 %copy-start = (bf16[196,768]{1,0:T(8,128)(2,1)S(1)}, bf16[196,768]{1,0:T(8,128)(2,1)}, u32[]{:S(2)}) copy-start(bf16[196,768]{1,0:T(8,128)(2,1)} %param.5) | copy-start | bytes 903172
  0.6 2.2 %copy-start.4 = (bf16[196,768]{1,0:T(8,128)(2,1)S(1)}, bf16[196,768]{1,0:T(8,128)(2,1)}, u32[]{:S(2)}) copy-start(bf16[196,768]{1,0:T(8,128)(2,1)} %param.6) | copy-start | bytes 903172
  119.7 2.9 %copy-start.3 = (bf16[32,8,768]{2,1,0:T(8,128)(2,1)S(1)}, bf16[32,8,768]{2,1,0:T(8,128)(2,1)}, u32[]{:S(2)}) copy-start(bf16[32,8,768]{2,1,0:T(8,128)(2,1)} %get-tuple-element.8) | copy-start | bytes 1179652
  122.4 24.3 %copy-start.2 = (bf16[2,768,768]{2,1,0:T(8,128)(2,1)S(1)}, bf16[2,768,768]{2,1,0:T(8,128)(2,1)}, u32[]{:S(2)}) copy-start(bf16[2,768,768]{2,1,0:T(8,128)(2,1)} %get-tuple-element.26) | copy-start | bytes 7077892
  146.7 2.5 %copy-start.1 = (bf16[2,768,768]{2,1,0:T(8,128)(2,1)S(1)}, bf16[2,768,768]{2,1,0:T(8,128)(2,1)}, u32[]{:S(2)}) copy-start(bf16[2,768,768]{2,1,0:T(8,128)(2,1)} %get-tuple-element.27) | copy-start | bytes 7077892

commit v3 on v2

--- a/solution.py
+++ b/solution.py
@@ -1,5 +1,3 @@
-import functools
-
 import jax
 import jax.numpy as jnp
 from jax import lax
@@ -8,7 +6,6 @@
 from jax.sharding import PartitionSpec as P
 
 D = 768
-SLOTS = 2
 TOK = 196
 PLANE = 32
 RING = 8
@@ -38,6 +35,10 @@
     return (lax.div(p, 8) * 16 + lax.div(z, 4) * 8 + lax.rem(p, 8), lax.rem(z, 4))
 
 
+def met():
+    pl.semaphore_wait(pltpu.get_barrier_semaphore(), PLANE + RING - 2)
+
+
 def remote(src, dst, send, recv, device):
     return pltpu.make_async_remote_copy(
         src_ref=src, dst_ref=dst, send_sem=send, recv_sem=recv, device_id=device, device_id_type=MESH
@@ -57,9 +58,8 @@
     lax.fori_loop(1, PLANE, one, 0)
     for offset in ring_offsets:
         pl.semaphore_signal(
-            barrier, inc=1, device_id=ring_device(p, (z + offset) % RING), device_id_type=MESH
+            barrier, inc=1, device_id=ring_device(p, lax.rem(z + offset, RING)), device_id_type=MESH
         )
-    pl.semaphore_wait(barrier, PLANE - 1 + len(ring_offsets))
 
 
 EVENTS = (
@@ -215,12 +215,14 @@
 
 
 def exchange_kernel(
-    sa, sb, win, wout,
-    out_a, out_b, gin, gout,
+    tokens, out_grad, router, win, wout,
+    token_grad, router_out, gin, gout,
+    rt, disp, comb, d_log, sa, sb, rs, rrcv, zs, zr,
     prcv, fs, rows, tout, ttr, part, rr, ofin, otr, psend, prcv2,
     w_in, w_out, g_in, g_out, act, slope, dpre, acc,
     w_sem, g_sem, ps_send, ps_recv, po_send, po_recv,
     z_send, in_recv, t_recv, out_recv, ot_recv,
+    pr_send, pr_recv, rz_send, rz_recv,
 ):
     p, zhi, h = place()
     z = zhi * 4 + h
@@ -230,8 +232,8 @@
         "z": z,
         "zhi": zhi,
         "up": up,
-        "h": ring_device(p, (z + step + RING) % RING),
-        "l": ring_device(p, (z - step + RING) % RING),
+        "h": ring_device(p, lax.rem(z + step + RING, RING)),
+        "l": ring_device(p, lax.rem(z - step + RING, RING)),
     }
     refs = {
         "rows": rows, "tout": tout, "ttr": ttr, "part": part, "rr": rr, "ofin": ofin, "otr": otr,
@@ -255,10 +257,24 @@
     ]
     for copy in w_copies:
         copy.start()
-    greet(p, zhi, h, (1, RING - 1))
+    greet(p, zhi, h, tuple(range(1, RING)))
+
+    natural = lax.broadcasted_iota(jnp.int32, (COLS, COLS), 0)
+    placed = lax.broadcasted_iota(jnp.int32, (COLS, COLS), 1)
+    source = (placed & 192) + ((placed & 4) << 3) + ((placed & 56) >> 1) + (placed & 3)
+    pick = jnp.where(natural == source, 1.0, 0.0).astype(BF)
+    rt[...] = jnp.dot(router[...], pick, preferred_element_type=F32).astype(BF)
+    logits = jnp.dot(tokens[...], rt[...], preferred_element_type=F32)
+    above = jnp.exp(logits - jnp.max(logits, axis=0, keepdims=True))
+    disp[...] = above / jnp.sum(above, axis=0, keepdims=True)
+    sa[...] = rounded_slots(disp[...].astype(BF), tokens[...])
+    met()
     sends = (sa, sb)
-    for t in (0, 1):
-        plane_start(p, zhi, h, sends[t], prcv.at[t], ps_send.at[t], ps_recv.at[t])
+    plane_start(p, zhi, h, sa, prcv.at[0], ps_send.at[0], ps_recv.at[0])
+    above = jnp.exp(logits - jnp.max(logits, axis=1, keepdims=True))
+    comb[...] = above / jnp.sum(above, axis=1, keepdims=True)
+    sb[...] = rounded_slots(comb[...].astype(BF), out_grad[...])
+    plane_start(p, zhi, h, sb, prcv.at[1], ps_send.at[1], ps_recv.at[1])
 
     def gather(t):
         plane_arrived(prcv.at[t], ps_recv.at[t])
@@ -369,17 +385,68 @@
     segment(len(EVENTS))
     plane_arrived(prcv2.at[0], po_recv.at[0])
     prcv2[0, p] = psend[0, p]
-    out_a[...] = prcv2[0]
+    slot_out = prcv2[0].astype(F32).reshape(COLS, D).astype(BF)
+    d_combine = across(out_grad[...], slot_out)
+    mixed = comb[...] * d_combine
+    d_log[...] = mixed - comb[...] * jnp.sum(mixed, axis=1, keepdims=True)
     plane_arrived(prcv2.at[1], po_recv.at[1])
     prcv2[1, p] = psend[1, p]
-    out_b[...] = prcv2[1]
+    slot_in_grad = prcv2[1].astype(F32).reshape(COLS, D).astype(BF)
+    d_dispatch = across(tokens[...], slot_in_grad)
+    mixed = disp[...] * d_dispatch
+    d_logits = (d_log[...] + (mixed - disp[...] * jnp.sum(mixed, axis=0, keepdims=True))).astype(BF)
+    rs[...] = rounded_slots(d_logits, tokens[...])
+    plane_start(p, zhi, h, rs, rrcv, pr_send, pr_recv)
+    token_grad[...] = (
+        jnp.dot(disp[...].astype(BF), slot_in_grad, preferred_element_type=F32) + across(d_logits, rt[...])
+    ).astype(BF)
+    plane_arrived(rrcv, pr_recv)
+    rrcv[p] = rs[p]
+    zs[...] = jnp.sum(rrcv[...].astype(F32), axis=0)
+    zr[z] = zs[:, pl.ds(window(h), COLS)]
+
+    def ring_copy(j, arrival):
+        to = lax.rem(z + j, RING)
+        slot = to if arrival else z
+        return remote(
+            zs.at[:, pl.ds(window(lax.rem(to, 4)), COLS)],
+            zr.at[slot],
+            rz_send.at[to],
+            rz_recv.at[slot],
+            ring_device(p, to),
+        )
+
+    for j in range(1, RING):
+        ring_copy(j, False).start()
+    for j in range(1, RING):
+        ring_copy(j, True).wait_recv()
+    total = jnp.sum(zr[...], axis=0)
+    total = jnp.where(zhi == 0, total[:4], total[4:])
+    router_out[...] = jnp.where(lax.rem(h, 2) == 0, total[:, :192], total[:, 64:])
+
     for t in (0, 1):
         plane_sent(prcv.at[t], ps_send.at[t])
         plane_sent(psend.at[t], po_send.at[t])
+    plane_sent(rrcv, pr_send)
+    for j in range(1, RING):
+        ring_copy(j, False).wait_send()
 
     both(lambda chains, table: chains.drain())
     for copy in g_copies:
         copy.wait()
+
+
+def rounded_slots(weights, values):
+    sums = lax.dot_general(weights, values, (((0,), (0,)), ((), ())), preferred_element_type=F32)
+    return sums.reshape(PLANE, 8, D).astype(BF)
+
+
+def across(left, right):
+    return lax.dot_general(left, right, (((1,), (1,)), ((), ())), preferred_element_type=F32)
+
+
+def window(h):
+    return pl.multiple_of((h + lax.div(h, 2)) * 128, 128)
 
 
 def plane_start(p, zhi, h, src, dst, send, recv):
@@ -401,7 +468,7 @@
     pltpu.make_async_copy(many, many, send).wait()
 
 
-def exchange(send_a, send_b, weight_in, weight_out):
+def layer(tokens, out_grad, slot_router, weight_in, weight_out):
     vmem = pl.BlockSpec(memory_space=pltpu.VMEM)
     anywhere = pl.BlockSpec(memory_space=pl.ANY)
     dma = pltpu.SemaphoreType.DMA
@@ -410,14 +477,24 @@
     return pl.pallas_call(
         exchange_kernel,
         out_shape=(
-            jax.ShapeDtypeStruct(send_a.shape, BF),
-            jax.ShapeDtypeStruct(send_a.shape, BF),
+            jax.ShapeDtypeStruct(tokens.shape, BF),
+            jax.ShapeDtypeStruct((4, 192), F32),
             jax.ShapeDtypeStruct(weight_in.shape, BF),
             jax.ShapeDtypeStruct(weight_out.shape, BF),
         ),
-        in_specs=[vmem, vmem, anywhere, anywhere],
+        in_specs=[vmem, vmem, vmem, anywhere, anywhere],
         out_specs=(vmem, vmem, anywhere, anywhere),
         scratch_shapes=[
+            pltpu.VMEM(slot_router.shape, BF),
+            pltpu.VMEM((TOK, COLS), F32),
+            pltpu.VMEM((TOK, COLS), F32),
+            pltpu.VMEM((TOK, COLS), F32),
+            pltpu.VMEM((PLANE, 8, D), BF),
+            pltpu.VMEM((PLANE, 8, D), BF),
+            pltpu.VMEM((PLANE, 8, D), BF),
+            pltpu.VMEM((PLANE, 8, D), BF),
+            pltpu.VMEM((8, D), F32),
+            pltpu.VMEM((RING, 8, COLS), F32),
             pltpu.VMEM((2, PLANE, 8, D), BF),
             pltpu.VMEM((LANES, COLS, 128), F32),
             pltpu.VMEM((2, RING, ROWS, D), BF),
@@ -433,10 +510,10 @@
             pltpu.VMEM(weight_out.shape, BF),
             pltpu.VMEM(weight_in.shape, BF),
             pltpu.VMEM(weight_out.shape, BF),
-            pltpu.VMEM((experts, RING * 64, width), BF),
-            pltpu.VMEM((experts, RING * 64, width), F32),
-            pltpu.VMEM((experts, RING * 64, width), BF),
-            pltpu.VMEM((RING * 64, D), F32),
+            pltpu.VMEM((experts, RING * HALF, width), BF),
+            pltpu.VMEM((experts, RING * HALF, width), F32),
+            pltpu.VMEM((experts, RING * HALF, width), BF),
+            pltpu.VMEM((RING * HALF, D), F32),
             dma((2,)),
             dma((2,)),
             dma((2,)),
@@ -448,100 +525,23 @@
             dma((4,)),
             dma((4, RING + 1)),
             dma((4, 2)),
-        ],
-        compiler_params=pltpu.CompilerParams(
-            collective_id=0, has_side_effects=True, vmem_limit_bytes=56 * 1024 * 1024
-        ),
-        name="exchange",
-    )(send_a, send_b, weight_in, weight_out)
-
-
-def window(h):
-    return pl.multiple_of((h + h // 2) * 128, 128)
-
-
-def router_kernel(rp, out, prcv, zs, zr, ps_send, ps_recv, z_send, z_recv):
-    p, zhi, h = place()
-    z = zhi * 4 + h
-    greet(p, zhi, h, tuple(range(1, RING)))
-
-    plane_start(p, zhi, h, rp, prcv, ps_send, ps_recv)
-    plane_arrived(prcv, ps_recv)
-    prcv[p] = rp[p]
-    zs[...] = jnp.sum(prcv[...].astype(F32), axis=0)
-    zr[z] = zs[:, pl.ds(window(h), COLS)]
-
-    def ring_copy(j, slot):
-        to = lax.rem(z + j, RING)
-        slot = z if slot is None else to
-        return remote(
-            zs.at[:, pl.ds(window(lax.rem(to, 4)), COLS)],
-            zr.at[slot],
-            z_send.at[to],
-            z_recv.at[slot],
-            ring_device(p, to),
-        )
-
-    for j in range(1, RING):
-        ring_copy(j, None).start()
-    for j in range(1, RING):
-        ring_copy(j, 1).wait_recv()
-    out[...] = jnp.sum(zr[...], axis=0)
-    plane_sent(rp, ps_send)
-    for j in range(1, RING):
-        ring_copy(j, None).wait_send()
-
-
-def router_reduce(partial):
-    vmem = pl.BlockSpec(memory_space=pltpu.VMEM)
-    dma = pltpu.SemaphoreType.DMA
-    return pl.pallas_call(
-        router_kernel,
-        out_shape=jax.ShapeDtypeStruct((8, COLS), F32),
-        in_specs=[vmem],
-        out_specs=vmem,
-        scratch_shapes=[
-            pltpu.VMEM((PLANE, 8, D), BF),
-            pltpu.VMEM((8, D), F32),
-            pltpu.VMEM((RING, 8, COLS), F32),
             dma(()),
             dma(()),
             dma((RING,)),
             dma((RING,)),
         ],
-        compiler_params=pltpu.CompilerParams(collective_id=1, has_side_effects=True),
-        name="router",
-    )(partial)
+        compiler_params=pltpu.CompilerParams(
+            collective_id=0, has_side_effects=True, vmem_limit_bytes=58 * 1024 * 1024
+        ),
+        name="layer",
+    )(tokens, out_grad, slot_router, weight_in, weight_out)
 
 
 def per_device(tokens, out_grad, slot_router, weight_in, weight_out):
-    router = slot_router.reshape(D, 4, 2, 8, 4).transpose(0, 1, 3, 2, 4).reshape(D, COLS)
-    logits = jnp.dot(tokens, router, preferred_element_type=F32)
-    dispatch = jax.nn.softmax(logits, axis=0)
-    combine = jax.nn.softmax(logits, axis=1)
-    dispatch16 = dispatch.astype(BF)
-    combine16 = combine.astype(BF)
-    slot_in = jnp.einsum("tc,td->cd", dispatch16, tokens, preferred_element_type=F32).astype(BF)
-    slot_grad = jnp.einsum("tc,td->cd", combine16, out_grad, preferred_element_type=F32).astype(BF)
-    slot_out, slot_in_grad, grad_first, grad_second = exchange(
-        slot_in.reshape(PLANE, 8, D), slot_grad.reshape(PLANE, 8, D), weight_in, weight_out
+    token_grad, router_grad, grad_first, grad_second = layer(
+        tokens, out_grad, slot_router, weight_in, weight_out
     )
-    slot_out = slot_out.reshape(COLS, D)
-    slot_in_grad = slot_in_grad.reshape(COLS, D)
-    d_combine = jnp.einsum("td,cd->tc", out_grad, slot_out, preferred_element_type=F32)
-    d_dispatch = jnp.einsum("td,cd->tc", tokens, slot_in_grad, preferred_element_type=F32)
-    from_combine = combine * (d_combine - jnp.sum(combine * d_combine, axis=1, keepdims=True))
-    from_dispatch = dispatch * (d_dispatch - jnp.sum(dispatch * d_dispatch, axis=0, keepdims=True))
-    d_logits = (from_combine + from_dispatch).astype(BF)
-    router_term = jnp.einsum("tc,td->cd", d_logits, tokens, preferred_element_type=F32).astype(BF)
-    router_sum = router_reduce(router_term.reshape(PLANE, 8, D))
-    token_grad = (
-        jnp.dot(dispatch16, slot_in_grad, preferred_element_type=F32)
-        + jnp.einsum("tc,dc->td", d_logits, router, preferred_element_type=F32)
-    ).astype(BF)
-    _, zhi, h = place()
-    router_grad = lax.dynamic_slice(router_sum, (zhi * 4, (h % 2) * 64), (4, 192)).T
-    return (token_grad, router_grad, grad_first, grad_second)
+    return (token_grad, router_grad.T, grad_first, grad_second)
 
 
 def solution(mesh):

time: 151 us -> 139 us (0.921)
  matrix products: 7.65 us -> 0 us
  Pallas kernels: 135 us -> 130 us
    dot_general x8 -> x0, matrix products: 7.65 us -> none  [the longest x1 1.4 us: per_device(): jnp.einsum('td,cd->tc', out_grad, slot_out, preferred_element_type=F32)]
    pallas_call x2 -> x1, Pallas kernels: 135 us -> 130 us  [layer(): pl.pallas_call(exchange_kernel, out_shape=(jax.ShapeDtypeStruct(tokens.sh...]
    unnamed x13 -> x6, local copies, waits for them, and re-layouts: 5.16 us -> 7.75 us
where the time goes in v3:
time: 139 us
  Pallas kernels  130 us (94%)
  local copies, waits for them, and re-layouts  7.75 us (6%)
    pallas_call x1, Pallas kernels, layer(): pl.pallas_call(exchange_kernel, out_shape=(jax.ShapeDtypeStruct(tokens.sh...  130 us
    unnamed x6, local copies, waits for them, and re-layouts  7.75 us

profile of v3, /device:TPU:1, one launch (start us, length us, event | category | flops | bytes accessed | tf_op | source)
XLA Modules:
  0.0 138.8 jit_solution(892814629896457023)
XLA Ops:
  0.6 130.4 %layer.1 = (bf16[196,768]{1,0:T(8,128)(2,1)}, f32[4,192]{1,0:T(4,128)}, bf16[2,768,768]{2,1,0:T(8,128)(2,1)}, bf16[2,768,768]{2,1,0:T(8,128)(2,1)}) custom-call(bf16[196,768]{1,0:T(8,128)(2,1)} %tokens.1, bf16[196,768]{1,0:T(8,128)(2,1)} %out_grad.1, bf16[768,256]{1,0:T(8,128)(2,1)} %router.1, bf16[2,768,768]{2,1,0:T(8,128)(2,1)} %win.1, ...), custom_call_target="tpu_custom_call" | custom-call | tf_op jit(solution)/shard_map/layer/pallas_call | solution.py:477
  131.0 1.7 %copy.13 = bf16[196,768]{1,0:T(8,128)(2,1)} copy(bf16[196,768]{1,0:T(8,128)(2,1)} %get-tuple-element.16) | data formatting | bytes 602112
  132.7 1.3 copy.14
  134.0 0.0 copy-start
  134.0 3.4 %copy.15 = bf16[2,768,768]{2,1,0:T(8,128)(2,1)} copy(bf16[2,768,768]{2,1,0:T(8,128)(2,1)} %get-tuple-element.18) | data formatting | bytes 4718592
  137.4 0.0 copy-done
  137.4 1.4 %copy.16 = bf16[2,768,768]{2,1,0:T(8,128)(2,1)} copy(bf16[2,768,768]{2,1,0:T(8,128)(2,1)S(1)} %copy-done) | data formatting | bytes 4718592
Async XLA Ops:
  134.0 3.4 %copy-start = (bf16[2,768,768]{2,1,0:T(8,128)(2,1)S(1)}, bf16[2,768,768]{2,1,0:T(8,128)(2,1)}, u32[]{:S(2)}) copy-start(bf16[2,768,768]{2,1,0:T(8,128)(2,1)} %get-tuple-element.19) | copy-start | bytes 7077892

commit v4 on v3

--- a/solution.py
+++ b/solution.py
@@ -215,12 +215,13 @@
 
 
 def exchange_kernel(
-    tokens, out_grad, router, win, wout,
-    token_grad, router_out, gin, gout,
+    tokens_in, out_grad_in, router_in, win, wout,
+    token_grad, router_out, g_in, g_out,
+    tokens, out_grad, router,
     rt, disp, comb, d_log, sa, sb, rs, rrcv, zs, zr,
     prcv, fs, rows, tout, ttr, part, rr, ofin, otr, psend, prcv2,
-    w_in, w_out, g_in, g_out, act, slope, dpre, acc,
-    w_sem, g_sem, ps_send, ps_recv, po_send, po_recv,
+    w_in, w_out, act, slope, dpre, acc,
+    a_sem, w_sem, ps_send, ps_recv, po_send, po_recv,
     z_send, in_recv, t_recv, out_recv, ot_recv,
     pr_send, pr_recv, rz_send, rz_recv,
 ):
@@ -251,6 +252,14 @@
         def _():
             body(inner, INNER)
 
+    a_copies = [
+        pltpu.make_async_copy(src, dst, a_sem.at[n])
+        for n, (src, dst) in enumerate(
+            ((router_in, router), (tokens_in, tokens), (out_grad_in, out_grad))
+        )
+    ]
+    for copy in a_copies:
+        copy.start()
     w_copies = [
         pltpu.make_async_copy(win, w_in, w_sem.at[0]),
         pltpu.make_async_copy(wout, w_out, w_sem.at[1]),
@@ -263,7 +272,9 @@
     placed = lax.broadcasted_iota(jnp.int32, (COLS, COLS), 1)
     source = (placed & 192) + ((placed & 4) << 3) + ((placed & 56) >> 1) + (placed & 3)
     pick = jnp.where(natural == source, 1.0, 0.0).astype(BF)
+    a_copies[0].wait()
     rt[...] = jnp.dot(router[...], pick, preferred_element_type=F32).astype(BF)
+    a_copies[1].wait()
     logits = jnp.dot(tokens[...], rt[...], preferred_element_type=F32)
     above = jnp.exp(logits - jnp.max(logits, axis=0, keepdims=True))
     disp[...] = above / jnp.sum(above, axis=0, keepdims=True)
@@ -271,6 +282,7 @@
     met()
     sends = (sa, sb)
     plane_start(p, zhi, h, sa, prcv.at[0], ps_send.at[0], ps_recv.at[0])
+    a_copies[2].wait()
     above = jnp.exp(logits - jnp.max(logits, axis=1, keepdims=True))
     comb[...] = above / jnp.sum(above, axis=1, keepdims=True)
     sb[...] = rounded_slots(comb[...].astype(BF), out_grad[...])
@@ -347,11 +359,6 @@
         g_in[e, :, span] = lax.dot_general(
             expert_rows(0, e), dpre[e, :, span], (((0,), (0,)), ((), ())), preferred_element_type=F32
         ).astype(BF)
-
-    g_copies = [
-        pltpu.make_async_copy(g_in, gin, g_sem.at[0]),
-        pltpu.make_async_copy(g_out, gout, g_sem.at[1]),
-    ]
 
     def segment(n):
         def body(chains, table):
@@ -377,9 +384,6 @@
                 (forward_piece if kind == "fwd" else backward_piece)(e, f)
         elif kind == "wg":
             weight_piece(*which)
-            if which == (1, 2):
-                for copy in g_copies:
-                    copy.start()
         else:
             out_last(which[0])
     segment(len(EVENTS))
@@ -432,8 +436,6 @@
         ring_copy(j, False).wait_send()
 
     both(lambda chains, table: chains.drain())
-    for copy in g_copies:
-        copy.wait()
 
 
 def rounded_slots(weights, values):
@@ -470,21 +472,23 @@
 
 def layer(tokens, out_grad, slot_router, weight_in, weight_out):
     vmem = pl.BlockSpec(memory_space=pltpu.VMEM)
-    anywhere = pl.BlockSpec(memory_space=pl.ANY)
     dma = pltpu.SemaphoreType.DMA
     experts = weight_in.shape[0]
     width = weight_in.shape[2]
     return pl.pallas_call(
         exchange_kernel,
         out_shape=(
-            jax.ShapeDtypeStruct(tokens.shape, BF),
-            jax.ShapeDtypeStruct((4, 192), F32),
-            jax.ShapeDtypeStruct(weight_in.shape, BF),
-            jax.ShapeDtypeStruct(weight_out.shape, BF),
+            pltpu.VMEM(tokens.shape, BF),
+            pltpu.VMEM((4, 192), F32),
+            pltpu.VMEM(weight_in.shape, BF),
+            pltpu.VMEM(weight_out.shape, BF),
         ),
-        in_specs=[vmem, vmem, vmem, anywhere, anywhere],
-        out_specs=(vmem, vmem, anywhere, anywhere),
+        in_specs=[pl.BlockSpec(memory_space=pltpu.HBM)] * 5,
+        out_specs=(vmem,) * 4,
         scratch_shapes=[
+            pltpu.VMEM(tokens.shape, BF),
+            pltpu.VMEM(out_grad.shape, BF),
+            pltpu.VMEM(slot_router.shape, BF),
             pltpu.VMEM(slot_router.shape, BF),
             pltpu.VMEM((TOK, COLS), F32),
             pltpu.VMEM((TOK, COLS), F32),
@@ -508,13 +512,11 @@
             pltpu.VMEM((2, PLANE, 8, D), BF),
             pltpu.VMEM(weight_in.shape, BF),
             pltpu.VMEM(weight_out.shape, BF),
-            pltpu.VMEM(weight_in.shape, BF),
-            pltpu.VMEM(weight_out.shape, BF),
             pltpu.VMEM((experts, RING * HALF, width), BF),
             pltpu.VMEM((experts, RING * HALF, width), F32),
             pltpu.VMEM((experts, RING * HALF, width), BF),
             pltpu.VMEM((RING * HALF, D), F32),
-            dma((2,)),
+            dma((3,)),
             dma((2,)),
             dma((2,)),
             dma((2,)),
@@ -531,15 +533,39 @@
             dma((RING,)),
         ],
         compiler_params=pltpu.CompilerParams(
-            collective_id=0, has_side_effects=True, vmem_limit_bytes=58 * 1024 * 1024
+            collective_id=0, has_side_effects=True, vmem_limit_bytes=61900000
         ),
         name="layer",
     )(tokens, out_grad, slot_router, weight_in, weight_out)
 
 
+def store_kernel(*refs):
+    count = len(refs) // 2
+    sems = refs[-1]
+    copies = [
+        pltpu.make_async_copy(refs[n], refs[count + n], sems.at[n]) for n in range(count)
+    ]
+    for copy in copies:
+        copy.start()
+    for copy in copies:
+        copy.wait()
+
+
+def store(*arrays):
+    return pl.pallas_call(
+        store_kernel,
+        out_shape=tuple(jax.ShapeDtypeStruct(a.shape, a.dtype) for a in arrays),
+        in_specs=[pl.BlockSpec(memory_space=pl.ANY)] * len(arrays),
+        out_specs=(pl.BlockSpec(memory_space=pltpu.HBM),) * len(arrays),
+        scratch_shapes=[pltpu.SemaphoreType.DMA((len(arrays),))],
+        compiler_params=pltpu.CompilerParams(vmem_limit_bytes=1024 * 1024),
+        name="store",
+    )(*arrays)
+
+
 def per_device(tokens, out_grad, slot_router, weight_in, weight_out):
-    token_grad, router_grad, grad_first, grad_second = layer(
-        tokens, out_grad, slot_router, weight_in, weight_out
+    token_grad, router_grad, grad_first, grad_second = store(
+        *layer(tokens, out_grad, slot_router, weight_in, weight_out)
     )
     return (token_grad, router_grad.T, grad_first, grad_second)
 

time: 139 us -> 132 us (0.950)
  local copies, waits for them, and re-layouts: 7.75 us -> 0 us
    unnamed x6 -> x0, local copies, waits for them, and re-layouts: 7.75 us -> none
    pallas_call x1 -> x2, Pallas kernels: 130 us -> 131 us  [the longest x1 129 us: layer(): pl.pallas_call(exchange_kernel, out_shape=(pltpu.VMEM(tokens.shape, BF),...]
where the time goes in v4:
time: 132 us
  Pallas kernels  131 us (99%)
    pallas_call x1, Pallas kernels, layer(): pl.pallas_call(exchange_kernel, out_shape=(pltpu.VMEM(tokens.shape, BF),...  129 us

profile of v4, /device:TPU:1, one launch (start us, length us, event | category | flops | bytes accessed | tf_op | source)
XLA Modules:
  0.0 131.7 jit_solution(1453563436890458703)
XLA Ops:
  0.6 128.5 %layer.1 = (bf16[196,768]{1,0:T(8,128)(2,1)S(1)}, f32[4,192]{1,0:T(4,128)S(1)}, bf16[2,768,768]{2,1,0:T(8,128)(2,1)S(1)}, bf16[2,768,768]{2,1,0:T(8,128)(2,1)S(1)}) custom-call(bf16[196,768]{1,0:T(8,128)(2,1)} %tokens_in.1, bf16[196,768]{1,0:T(8,128)(2,1)} %out_grad_in.1, bf16[768,256]{1,0:T(8,128)(2,1)} %router_in.1, bf16[2,768,768]{2,1,0:T(8,128)(2,1)} %win.1, ...), custom_call_target="tpu_custom_call" | custom-call | tf_op jit(solution)/shard_map/layer/pallas_call | solution.py:478
  129.2 2.3 %store.1 = (bf16[196,768]{1,0:T(8,128)(2,1)}, f32[4,192]{1,0:T(4,128)}, bf16[2,768,768]{2,1,0:T(8,128)(2,1)}, bf16[2,768,768]{2,1,0:T(8,128)(2,1)}) custom-call(bf16[196,768]{1,0:T(8,128)(2,1)S(1)} %get-tuple-element.12.refs_0_, f32[4,192]{1,0:T(4,128)S(1)} %get-tuple-element.13.refs_1_, bf16[2,768,768]{2,1,0:T(8,128)(2,1)S(1)} %get-tuple-element.14.refs_2_, ...), custom_call_target="tpu_custom_call" | custom-call | tf_op jit(solution)/shard_map/store/pallas_call | solution.py:555

commit v5 on v4

--- a/solution.py
+++ b/solution.py
@@ -64,13 +64,21 @@
 
 EVENTS = (
     ("gather",),
-    ("fwd", 0),
-    ("fwd", 1),
-    ("bwd", 0),
+    ("fwd", 0, 0),
+    ("fwd", 0, 1),
+    ("fwd", 0, 2),
+    ("fwd", 1, 0),
+    ("fwd", 1, 1),
+    ("fwd", 1, 2),
+    ("bwd", 0, 0),
+    ("bwd", 0, 1),
+    ("bwd", 0, 2),
     ("wg", 0, 0),
     ("wg", 0, 1),
     ("wg", 0, 2),
-    ("bwd", 1),
+    ("bwd", 1, 0),
+    ("bwd", 1, 1),
+    ("bwd", 1, 2),
     ("wg", 1, 0),
     ("wg", 1, 1),
     ("wg", 1, 2),
@@ -78,35 +86,51 @@
     ("last", 1),
 )
 EDGE = (
-    (("io", 0, "l", 0), ("iO", 0, "h", 3), ("io", 1, "l", 0), ("iO", 1, "h", 3)),
-    (("iX", 0, "l", 3), ("ix", 0, "h", 2), ("iX", 1, "l", 3), ("iO", 2, "h", 3), ("iX", 0, "l", 2), ("iO", 3, "h", 3), ("ix", 1, "h", 2), ("iX", 2, "l", 3), ("io", 2, "l", 0), ("iX", 1, "l", 2), ("iX", 3, "l", 3), ("io", 3, "l", 0)),
-    (("oX", 0, "h", 2), ("oX", 0, "h", 3), ("oo", 0, "h", 0)),
-    (("oo", 0, "h", 1), ("ix", 2, "h", 2), ("oo", 0, "h", 2), ("oX", 1, "h", 2), ("iX", 2, "l", 2), ("oX", 1, "h", 3), ("oo", 1, "h", 0), ("ix", 3, "h", 2), ("oo", 1, "h", 1), ("oo", 1, "h", 2), ("oX", 0, "l", 2), ("iX", 3, "l", 2), ("oX", 0, "l", 3), ("oT", 0, "h", 2)),
+    (("io", 0, "l", 0), ("io", 1, "l", 0), ("iO", 0, "h", 3), ("iO", 1, "h", 3), ("ix", 0, "h", 2), ("iX", 0, "l", 3)),
+    (("iX", 1, "l", 3), ("iO", 2, "h", 3), ("iX", 0, "l", 2), ("iO", 3, "h", 3), ("ix", 1, "h", 2), ("iX", 2, "l", 3), ("io", 3, "l", 0), ("iX", 1, "l", 2), ("io", 2, "l", 0), ("iX", 3, "l", 3)),
+    (),
+    (),
+    (("oo", 0, "h", 0), ("oX", 0, "h", 2), ("ix", 2, "h", 2), ("iX", 2, "l", 2), ("oX", 0, "h", 3), ("ix", 3, "h", 2), ("iX", 3, "l", 2), ("oo", 0, "h", 1)),
+    (),
+    (("oo", 0, "h", 2),),
+    (("oX", 1, "h", 2), ("oo", 1, "h", 1), ("oX", 1, "h", 3)),
+    (),
+    (),
+    (("oo", 1, "h", 2), ("oo", 1, "h", 0), ("oo", 2, "h", 0)),
+    (),
     (("oX", 2, "h", 2),),
     (("oX", 2, "h", 3),),
-    (("oo", 2, "h", 0),),
+    (),
+    (),
+    (("oX", 3, "h", 2), ("oX", 0, "l", 3), ("oo", 3, "h", 0), ("oX", 0, "l", 2), ("oX", 3, "h", 3)),
+    (("oo", 2, "h", 2), ("oX", 1, "l", 2), ("oX", 1, "l", 3)),
+    (("oT", 0, "h", 2), ("oT", 1, "h", 2)),
     (("oo", 2, "h", 1),),
-    (("oo", 2, "h", 2),),
-    (("oX", 3, "h", 2), ("oX", 1, "l", 2)),
-    (("oX", 3, "h", 3), ("oX", 1, "l", 3)),
-    (("oT", 1, "h", 2), ("oo", 3, "h", 0)),
-    (("oX", 2, "l", 2), ("oo", 3, "h", 1), ("oX", 2, "l", 3), ("oT", 2, "h", 2), ("oo", 3, "h", 2), ("oX", 3, "l", 2), ("oX", 3, "l", 3), ("oT", 3, "h", 2)),
+    (("oX", 2, "l", 2), ("oo", 3, "h", 1), ("oo", 3, "h", 2), ("oX", 3, "l", 2), ("oX", 2, "l", 3), ("oT", 2, "h", 2), ("oX", 3, "l", 3), ("oT", 3, "h", 2)),
     (),
 )
 INNER = (
-    (("io", 0, "l", 1), ("iy", 0, "h", 2), ("io", 0, "h", 2), ("io", 1, "l", 1)),
-    (("io", 0, "h", 1), ("io", 0, "l", 0), ("io", 1, "l", 0), ("iy", 1, "h", 2), ("io", 0, "h", 0), ("iX", 0, "l", 3), ("io", 1, "h", 0), ("iX", 1, "l", 3), ("iX", 0, "h", 3), ("iX", 0, "l", 2), ("iX", 1, "h", 3), ("iX", 2, "l", 3)),
-    (("iX", 0, "h", 2), ("io", 2, "l", 0), ("io", 1, "h", 1), ("iX", 1, "l", 2), ("io", 1, "h", 2), ("io", 2, "l", 1)),
-    (("iX", 1, "h", 2), ("iX", 3, "l", 3), ("iy", 2, "h", 2), ("io", 3, "l", 0), ("oX", 0, "h", 2), ("iX", 2, "h", 3), ("oX", 0, "h", 3), ("io", 2, "h", 0), ("io", 2, "h", 1), ("io", 3, "l", 1), ("oo", 0, "h", 0), ("io", 2, "h", 2), ("oo", 0, "h", 1), ("iy", 3, "h", 2), ("oX", 1, "h", 2), ("iX", 3, "h", 3), ("oX", 0, "l", 2), ("iX", 2, "l", 2), ("oX", 0, "l", 3), ("oX", 1, "h", 3)),
-    (("oo", 1, "h", 0), ("iX", 2, "h", 2), ("oo", 1, "h", 1), ("io", 3, "h", 0)),
-    (("io", 3, "h", 1), ("iX", 3, "l", 2)),
-    (("io", 3, "h", 2),),
-    (),
-    (("iX", 3, "h", 2), ("oX", 2, "h", 2), ("oo", 0, "l", 0), ("oX", 2, "h", 3)),
-    (("oX", 1, "l", 2),),
-    (("oo", 2, "h", 0), ("oX", 1, "l", 3)),
-    (("oo", 2, "h", 1), ("oo", 1, "l", 0), ("oX", 2, "l", 2), ("oX", 3, "h", 2), ("oX", 2, "l", 3), ("oX", 3, "h", 3), ("oo", 2, "l", 0)),
-    (("oX", 3, "l", 2), ("oo", 3, "h", 0), ("oX", 3, "l", 3), ("oo", 3, "h", 1), ("oo", 3, "l", 0)),
+    (("iy", 0, "h", 2), ("iy", 1, "h", 2), ("io", 0, "l", 1), ("io", 0, "h", 2), ("io", 1, "l", 1), ("io", 0, "l", 0), ("io", 0, "h", 1), ("io", 1, "l", 0), ("io", 0, "h", 0), ("iX", 0, "l", 3), ("io", 1, "h", 0), ("iX", 1, "l", 3), ("iX", 0, "l", 2), ("iX", 0, "h", 3)),
+    (("iX", 1, "h", 3), ("iX", 0, "h", 2), ("iy", 2, "h", 2), ("io", 1, "h", 2), ("iy", 3, "h", 2), ("io", 3, "l", 1), ("iX", 1, "l", 2), ("io", 2, "l", 0), ("io", 1, "h", 1)),
+    (("iX", 2, "l", 3),),
+    (),
+    (("io", 3, "l", 0), ("io", 2, "l", 1), ("iX", 1, "h", 2)),
+    (("io", 2, "h", 0),),
+    (("io", 2, "h", 2), ("io", 2, "h", 1), ("iX", 2, "l", 2), ("iX", 2, "h", 3), ("iX", 3, "l", 3)),
+    (("oX", 0, "h", 2), ("iX", 2, "h", 2), ("oo", 0, "h", 0)),
+    (("iX", 3, "h", 3), ("iX", 3, "l", 2), ("oX", 0, "h", 3), ("io", 3, "h", 0), ("io", 3, "h", 1), ("iX", 3, "h", 2), ("oX", 1, "h", 2)),
+    (("io", 3, "h", 2), ("oo", 1, "h", 1), ("oX", 1, "h", 3)),
+    (),
+    (("oX", 0, "l", 3),),
+    (),
+    (),
+    (("oX", 0, "l", 2),),
+    (("oo", 1, "h", 0), ("oX", 1, "l", 2), ("oX", 1, "l", 3), ("oX", 2, "h", 2)),
+    (("oo", 1, "l", 0), ("oo", 0, "l", 0)),
+    (("oo", 0, "h", 1), ("oX", 2, "h", 3), ("oX", 3, "h", 2), ("oX", 3, "h", 3), ("oX", 2, "l", 2)),
+    (("oX", 3, "l", 2), ("oo", 2, "h", 0)),
+    (("oo", 3, "h", 0), ("oX", 2, "l", 3), ("oX", 3, "l", 3)),
+    (("oo", 2, "l", 0), ("oo", 2, "h", 1), ("oo", 3, "l", 0), ("oo", 3, "h", 1)),
     (),
 )
 
@@ -374,14 +398,14 @@
         if kind == "gather":
             gather(1)
         elif kind in ("fwd", "bwd"):
-            (e,) = which
+            e, f = which
             q = e if kind == "fwd" else 2 + e
-            both(lambda chains, table, q=q: chains.all_rows(q))
-            if q == 0:
+            if f == 0:
+                both(lambda chains, table, q=q: chains.all_rows(q))
+            if (q, f) == (0, 0):
                 for copy in w_copies:
                     copy.wait()
-            for f in range(3):
-                (forward_piece if kind == "fwd" else backward_piece)(e, f)
+            (forward_piece if kind == "fwd" else backward_piece)(e, f)
         elif kind == "wg":
             weight_piece(*which)
         else:

time: 132 us -> 124 us (0.939)
  Pallas kernels: 131 us -> 123 us
    pallas_call x1, Pallas kernels: 129 us -> 121 us  [layer(): pl.pallas_call(exchange_kernel, out_shape=(pltpu.VMEM(tokens.shape, BF),...]
where the time goes in v5:
time: 124 us
  Pallas kernels  123 us (99%)
    pallas_call x1, Pallas kernels, layer(): pl.pallas_call(exchange_kernel, out_shape=(pltpu.VMEM(tokens.shape, BF),...  121 us

profile of v5, /device:TPU:1, one launch (start us, length us, event | category | flops | bytes accessed | tf_op | source)
XLA Modules:
  0.0 123.9 jit_solution(1088102503783212555)
XLA Ops:
  0.6 120.8 %layer.1 = (bf16[196,768]{1,0:T(8,128)(2,1)S(1)}, f32[4,192]{1,0:T(4,128)S(1)}, bf16[2,768,768]{2,1,0:T(8,128)(2,1)S(1)}, bf16[2,768,768]{2,1,0:T(8,128)(2,1)S(1)}) custom-call(bf16[196,768]{1,0:T(8,128)(2,1)} %tokens_in.1, bf16[196,768]{1,0:T(8,128)(2,1)} %out_grad_in.1, bf16[768,256]{1,0:T(8,128)(2,1)} %router_in.1, bf16[2,768,768]{2,1,0:T(8,128)(2,1)} %win.1, ...), custom_call_target="tpu_custom_call" | custom-call | tf_op jit(solution)/shard_map/layer/pallas_call | solution.py:502
  121.4 2.3 %store.1 = (bf16[196,768]{1,0:T(8,128)(2,1)}, f32[4,192]{1,0:T(4,128)}, bf16[2,768,768]{2,1,0:T(8,128)(2,1)}, bf16[2,768,768]{2,1,0:T(8,128)(2,1)}) custom-call(bf16[196,768]{1,0:T(8,128)(2,1)S(1)} %get-tuple-element.12.refs_0_, f32[4,192]{1,0:T(4,128)S(1)} %get-tuple-element.13.refs_1_, bf16[2,768,768]{2,1,0:T(8,128)(2,1)S(1)} %get-tuple-element.14.refs_2_, ...), custom_call_target="tpu_custom_call" | custom-call | tf_op jit(solution)/shard_map/store/pallas_call | solution.py:579

commit v6 on v5

--- a/solution.py
+++ b/solution.py
@@ -86,51 +86,51 @@
     ("last", 1),
 )
 EDGE = (
-    (("io", 0, "l", 0), ("io", 1, "l", 0), ("iO", 0, "h", 3), ("iO", 1, "h", 3), ("ix", 0, "h", 2), ("iX", 0, "l", 3)),
-    (("iX", 1, "l", 3), ("iO", 2, "h", 3), ("iX", 0, "l", 2), ("iO", 3, "h", 3), ("ix", 1, "h", 2), ("iX", 2, "l", 3), ("io", 3, "l", 0), ("iX", 1, "l", 2), ("io", 2, "l", 0), ("iX", 3, "l", 3)),
-    (),
-    (),
-    (("oo", 0, "h", 0), ("oX", 0, "h", 2), ("ix", 2, "h", 2), ("iX", 2, "l", 2), ("oX", 0, "h", 3), ("ix", 3, "h", 2), ("iX", 3, "l", 2), ("oo", 0, "h", 1)),
-    (),
-    (("oo", 0, "h", 2),),
-    (("oX", 1, "h", 2), ("oo", 1, "h", 1), ("oX", 1, "h", 3)),
-    (),
-    (),
-    (("oo", 1, "h", 2), ("oo", 1, "h", 0), ("oo", 2, "h", 0)),
-    (),
-    (("oX", 2, "h", 2),),
-    (("oX", 2, "h", 3),),
-    (),
-    (),
-    (("oX", 3, "h", 2), ("oX", 0, "l", 3), ("oo", 3, "h", 0), ("oX", 0, "l", 2), ("oX", 3, "h", 3)),
-    (("oo", 2, "h", 2), ("oX", 1, "l", 2), ("oX", 1, "l", 3)),
-    (("oT", 0, "h", 2), ("oT", 1, "h", 2)),
-    (("oo", 2, "h", 1),),
-    (("oX", 2, "l", 2), ("oo", 3, "h", 1), ("oo", 3, "h", 2), ("oX", 3, "l", 2), ("oX", 2, "l", 3), ("oT", 2, "h", 2), ("oX", 3, "l", 3), ("oT", 3, "h", 2)),
+    (("io", 0, "l", 0), ("io", 1, "l", 0), ("iO", 0, "h", 3), ("iO", 1, "h", 3), ("ix", 0, "h", 2), ("iX", 0, "l", 3), ("ix", 1, "h", 2), ("iX", 1, "l", 3), ("iX", 0, "l", 2)),
+    (("iO", 2, "h", 3), ("io", 3, "l", 0), ("iX", 1, "l", 2), ("iO", 3, "h", 3), ("ix", 2, "h", 2), ("io", 2, "l", 0), ("iX", 2, "l", 3), ("iX", 2, "l", 2), ("iX", 3, "l", 3)),
+    (),
+    (),
+    (("oX", 0, "h", 3), ("oo", 0, "h", 2), ("ix", 3, "h", 2), ("oX", 0, "h", 2), ("iX", 3, "l", 2), ("oo", 0, "h", 0)),
+    (("oo", 0, "h", 1),),
+    (),
+    (("oX", 1, "h", 2), ("oo", 1, "h", 1), ("oo", 1, "h", 0), ("oX", 1, "h", 3)),
+    (),
+    (),
+    (("oX", 2, "h", 3), ("oo", 2, "h", 0)),
+    (("oX", 0, "l", 2), ("oX", 2, "h", 2)),
+    (("oo", 1, "h", 2), ("oo", 2, "h", 1)),
+    (("oT", 0, "h", 2),),
+    (),
+    (),
+    (("oX", 3, "h", 2),),
+    (("oX", 3, "h", 3), ("oX", 1, "l", 2), ("oo", 3, "h", 0)),
+    (("oX", 1, "l", 3), ("oX", 0, "l", 3), ("oT", 1, "h", 2), ("oo", 2, "h", 2), ("oo", 3, "h", 2), ("oX", 2, "l", 2), ("oo", 3, "h", 1), ("oX", 2, "l", 3), ("oX", 3, "l", 2)),
+    (("oT", 2, "h", 2), ("oX", 3, "l", 3), ("oT", 3, "h", 2)),
+    (),
     (),
 )
 INNER = (
-    (("iy", 0, "h", 2), ("iy", 1, "h", 2), ("io", 0, "l", 1), ("io", 0, "h", 2), ("io", 1, "l", 1), ("io", 0, "l", 0), ("io", 0, "h", 1), ("io", 1, "l", 0), ("io", 0, "h", 0), ("iX", 0, "l", 3), ("io", 1, "h", 0), ("iX", 1, "l", 3), ("iX", 0, "l", 2), ("iX", 0, "h", 3)),
-    (("iX", 1, "h", 3), ("iX", 0, "h", 2), ("iy", 2, "h", 2), ("io", 1, "h", 2), ("iy", 3, "h", 2), ("io", 3, "l", 1), ("iX", 1, "l", 2), ("io", 2, "l", 0), ("io", 1, "h", 1)),
-    (("iX", 2, "l", 3),),
-    (),
-    (("io", 3, "l", 0), ("io", 2, "l", 1), ("iX", 1, "h", 2)),
-    (("io", 2, "h", 0),),
-    (("io", 2, "h", 2), ("io", 2, "h", 1), ("iX", 2, "l", 2), ("iX", 2, "h", 3), ("iX", 3, "l", 3)),
-    (("oX", 0, "h", 2), ("iX", 2, "h", 2), ("oo", 0, "h", 0)),
-    (("iX", 3, "h", 3), ("iX", 3, "l", 2), ("oX", 0, "h", 3), ("io", 3, "h", 0), ("io", 3, "h", 1), ("iX", 3, "h", 2), ("oX", 1, "h", 2)),
-    (("io", 3, "h", 2), ("oo", 1, "h", 1), ("oX", 1, "h", 3)),
-    (),
-    (("oX", 0, "l", 3),),
-    (),
-    (),
-    (("oX", 0, "l", 2),),
-    (("oo", 1, "h", 0), ("oX", 1, "l", 2), ("oX", 1, "l", 3), ("oX", 2, "h", 2)),
-    (("oo", 1, "l", 0), ("oo", 0, "l", 0)),
-    (("oo", 0, "h", 1), ("oX", 2, "h", 3), ("oX", 3, "h", 2), ("oX", 3, "h", 3), ("oX", 2, "l", 2)),
-    (("oX", 3, "l", 2), ("oo", 2, "h", 0)),
-    (("oo", 3, "h", 0), ("oX", 2, "l", 3), ("oX", 3, "l", 3)),
-    (("oo", 2, "l", 0), ("oo", 2, "h", 1), ("oo", 3, "l", 0), ("oo", 3, "h", 1)),
+    (("iy", 0, "h", 2), ("iy", 1, "h", 2), ("io", 0, "l", 1), ("io", 0, "l", 0), ("io", 1, "h", 2), ("io", 0, "h", 2), ("io", 1, "l", 0), ("io", 1, "l", 1)),
+    (("io", 0, "h", 1), ("iy", 2, "h", 2), ("iX", 0, "l", 3), ("io", 0, "h", 0), ("iX", 0, "l", 2), ("io", 3, "l", 1), ("iX", 0, "h", 3), ("io", 2, "l", 1), ("iX", 0, "h", 2)),
+    (("iy", 3, "h", 2), ("iX", 1, "l", 2), ("iX", 1, "l", 3)),
+    (("io", 2, "l", 0), ("io", 1, "h", 1), ("iX", 2, "l", 3)),
+    (("iX", 1, "h", 2), ("iX", 2, "l", 2), ("io", 1, "h", 0), ("iX", 1, "h", 3), ("io", 2, "h", 2)),
+    (("io", 3, "l", 0),),
+    (("io", 2, "h", 1), ("oX", 0, "h", 3)),
+    (("io", 2, "h", 0), ("iX", 2, "h", 3), ("iX", 3, "l", 2), ("oX", 0, "h", 2), ("oo", 0, "h", 0), ("iX", 3, "l", 3), ("iX", 2, "h", 2), ("io", 3, "h", 0), ("oX", 0, "l", 2)),
+    (("oX", 1, "h", 2), ("oo", 0, "h", 1)),
+    (("io", 3, "h", 1),),
+    (("iX", 3, "h", 2), ("iX", 3, "h", 3)),
+    (("oX", 1, "h", 3),),
+    (("io", 3, "h", 2), ("oo", 1, "h", 0), ("oX", 2, "h", 3), ("oX", 1, "l", 2)),
+    (("oX", 2, "h", 2), ("oX", 1, "l", 3)),
+    (("oo", 2, "h", 0), ("oX", 0, "l", 3), ("oo", 2, "h", 1), ("oX", 2, "l", 2), ("oo", 1, "h", 1)),
+    (),
+    (),
+    (("oX", 2, "l", 3), ("oX", 3, "h", 2)),
+    (("oo", 0, "l", 0), ("oX", 3, "h", 3), ("oX", 3, "l", 2), ("oo", 3, "h", 0)),
+    (("oX", 3, "l", 3), ("oo", 1, "l", 0)),
+    (("oo", 3, "l", 0), ("oo", 2, "l", 0), ("oo", 3, "h", 1)),
     (),
 )
 
@@ -428,6 +428,10 @@
     token_grad[...] = (
         jnp.dot(disp[...].astype(BF), slot_in_grad, preferred_element_type=F32) + across(d_logits, rt[...])
     ).astype(BF)
+    for t in (0, 1):
+        plane_sent(prcv.at[t], ps_send.at[t])
+        plane_sent(psend.at[t], po_send.at[t])
+    both(lambda chains, table: chains.drain())
     plane_arrived(rrcv, pr_recv)
     rrcv[p] = rs[p]
     zs[...] = jnp.sum(rrcv[...].astype(F32), axis=0)
@@ -444,7 +448,7 @@
             ring_device(p, to),
         )
 
-    for j in range(1, RING):
+    for j in (4, 3, 5, 2, 6, 1, 7):
         ring_copy(j, False).start()
     for j in range(1, RING):
         ring_copy(j, True).wait_recv()
@@ -452,15 +456,10 @@
     total = jnp.where(zhi == 0, total[:4], total[4:])
     router_out[...] = jnp.where(lax.rem(h, 2) == 0, total[:, :192], total[:, 64:])
 
-    for t in (0, 1):
-        plane_sent(prcv.at[t], ps_send.at[t])
-        plane_sent(psend.at[t], po_send.at[t])
     plane_sent(rrcv, pr_send)
     for j in range(1, RING):
         ring_copy(j, False).wait_send()
 
-    both(lambda chains, table: chains.drain())
-
 
 def rounded_slots(weights, values):
     sums = lax.dot_general(weights, values, (((0,), (0,)), ((), ())), preferred_element_type=F32)
@@ -475,13 +474,24 @@
     return pl.multiple_of((h + lax.div(h, 2)) * 128, 128)
 
 
+def far(k):
+    return min(k, 4 - k)
+
+
+OFFSETS = sorted(
+    ((dy, dx, dc) for dy in range(4) for dx in range(4) for dc in (0, 1) if (dy, dx, dc) != (0, 0, 0)),
+    key=lambda o: (-far(o[0]) - far(o[1]), o[2], (o[0] + o[1]) % 2, o),
+)
+
+
 def plane_start(p, zhi, h, src, dst, send, recv):
-    def step(j, carry):
-        q = lax.rem(p + j, PLANE)
-        remote(src.at[q], dst.at[p], send, recv, plane_device(q, zhi, h)).start()
-        return carry
-
-    lax.fori_loop(1, PLANE, step, 0)
+    y, x, core = lax.div(p, 8), lax.rem(lax.div(p, 2), 4), lax.rem(p, 2)
+    for dy, dx, dc in OFFSETS:
+        to_y, to_x = lax.rem(y + dy, 4), lax.rem(x + dx, 4)
+        to_core = 1 - core if dc else core
+        q = to_y * 8 + to_x * 2 + to_core
+        device = (to_y * 16 + zhi * 8 + to_x * 2 + to_core, h)
+        remote(src.at[q], dst.at[p], send, recv, device).start()
 
 
 def plane_arrived(dst, recv):

time: 124 us -> 122 us (0.984)
    pallas_call x1, Pallas kernels: 121 us -> 119 us  [layer(): pl.pallas_call(exchange_kernel, out_shape=(pltpu.VMEM(tokens.shape, BF),...]
where the time goes in v6:
time: 122 us
  Pallas kernels  122 us (100%)
    pallas_call x1, Pallas kernels, layer(): pl.pallas_call(exchange_kernel, out_shape=(pltpu.VMEM(tokens.shape, BF),...  119 us

profile of v6, /device:TPU:1, one launch (start us, length us, event | category | flops | bytes accessed | tf_op | source)
XLA Modules:
  0.0 122.4 jit_solution(1774533771703380214)
XLA Ops:
  0.6 119.2 %layer.1 = (bf16[196,768]{1,0:T(8,128)(2,1)S(1)}, f32[4,192]{1,0:T(4,128)S(1)}, bf16[2,768,768]{2,1,0:T(8,128)(2,1)S(1)}, bf16[2,768,768]{2,1,0:T(8,128)(2,1)S(1)}) custom-call(bf16[196,768]{1,0:T(8,128)(2,1)} %tokens_in.1, bf16[196,768]{1,0:T(8,128)(2,1)} %out_grad_in.1, bf16[768,256]{1,0:T(8,128)(2,1)} %router_in.1, bf16[2,768,768]{2,1,0:T(8,128)(2,1)} %win.1, ...), custom_call_target="tpu_custom_call" | custom-call | tf_op jit(solution)/shard_map/layer/pallas_call | solution.py:512
  119.9 2.3 %store.1 = (bf16[196,768]{1,0:T(8,128)(2,1)}, f32[4,192]{1,0:T(4,128)}, bf16[2,768,768]{2,1,0:T(8,128)(2,1)}, bf16[2,768,768]{2,1,0:T(8,128)(2,1)}) custom-call(bf16[196,768]{1,0:T(8,128)(2,1)S(1)} %get-tuple-element.12.refs_0_, f32[4,192]{1,0:T(4,128)S(1)} %get-tuple-element.13.refs_1_, bf16[2,768,768]{2,1,0:T(8,128)(2,1)S(1)} %get-tuple-element.14.refs_2_, ...), custom_call_target="tpu_custom_call" | custom-call | tf_op jit(solution)/shard_map/store/pallas_call | solution.py:589

commit v7 on v6

--- a/solution.py
+++ b/solution.py
@@ -13,6 +13,7 @@
 COLS = 256
 HALF = 64
 COPIES = 80
+FIRST = 3
 LANES = 6
 MESH = pl.DeviceIdType.MESH
 BF = jnp.bfloat16
@@ -310,7 +311,6 @@
     above = jnp.exp(logits - jnp.max(logits, axis=1, keepdims=True))
     comb[...] = above / jnp.sum(above, axis=1, keepdims=True)
     sb[...] = rounded_slots(comb[...].astype(BF), out_grad[...])
-    plane_start(p, zhi, h, sb, prcv.at[1], ps_send.at[1], ps_recv.at[1])
 
     def gather(t):
         plane_arrived(prcv.at[t], ps_recv.at[t])
@@ -326,18 +326,16 @@
                 tout[t, piece, lanes] = other.astype(BF)
 
     def out_last(t):
-        def finish(chains, table):
-            for e in (0, 1):
-                chains.finish(2 * t + e)
-
-        both(finish)
+        for e in (0, 1):
+            both(lambda chains, table, e=e: chains.finish(2 * t + e))
+            for c in range(LANES):
+                lanes = slice(c * 128, (c + 1) * 128)
+                for s in (2 * e, 2 * e + 1):
+                    piece = slice(s * PLANE, (s + 1) * PLANE)
+                    fs[c, pl.ds(zhi * 4 + s, PLANE, stride=8), :] = part[t, z, piece, lanes].astype(F32)
+                    fs[c, pl.ds((1 - zhi) * 4 + s, PLANE, stride=8), :] = ofin[t, piece, lanes].astype(F32)
         for c in range(LANES):
-            lanes = slice(c * 128, (c + 1) * 128)
-            for s in range(4):
-                piece = slice(s * PLANE, (s + 1) * PLANE)
-                fs[c, pl.ds(zhi * 4 + s, PLANE, stride=8), :] = part[t, z, piece, lanes].astype(F32)
-                fs[c, pl.ds((1 - zhi) * 4 + s, PLANE, stride=8), :] = ofin[t, piece, lanes].astype(F32)
-            psend[t, :, :, lanes] = fs[c].reshape(PLANE, 8, 128).astype(BF)
+            psend[t, :, :, c * 128 : (c + 1) * 128] = fs[c].reshape(PLANE, 8, 128).astype(BF)
         plane_start(p, zhi, h, psend.at[t], prcv2.at[t], po_send.at[t], po_recv.at[t])
 
 
@@ -384,16 +382,21 @@
             expert_rows(0, e), dpre[e, :, span], (((0,), (0,)), ((), ())), preferred_element_type=F32
         ).astype(BF)
 
-    def segment(n):
+    def segment(n, span=slice(None)):
         def body(chains, table):
-            for item in table[n]:
+            for item in table[n][span]:
                 chains.emit(*item)
 
         both(body)
 
     gather(0)
     for n, event in enumerate(EVENTS):
-        segment(n)
+        if n == 0:
+            segment(0, slice(0, FIRST))
+            plane_start(p, zhi, h, sb, prcv.at[1], ps_send.at[1], ps_recv.at[1])
+            segment(0, slice(FIRST, None))
+        else:
+            segment(n)
         kind, which = event[0], event[1:]
         if kind == "gather":
             gather(1)

time: 122 us -> 121 us (level)
  Pallas kernels: 122 us -> 120 us
    pallas_call x1, Pallas kernels: 119 us -> 117 us  [layer(): pl.pallas_call(exchange_kernel, out_shape=(pltpu.VMEM(tokens.shape, BF),...]
where the time goes in v7:
time: 121 us; the launch traced here: 120 us
  Pallas kernels  120 us (99%)
    pallas_call x1, Pallas kernels, layer(): pl.pallas_call(exchange_kernel, out_shape=(pltpu.VMEM(tokens.shape, BF),...  117 us

profile of v7, /device:TPU:1, one launch (start us, length us, event | category | flops | bytes accessed | tf_op | source)
XLA Modules:
  0.0 120.5 jit_solution(15549502559770637290)
XLA Ops:
  0.6 117.3 %layer.1 = (bf16[196,768]{1,0:T(8,128)(2,1)S(1)}, f32[4,192]{1,0:T(4,128)S(1)}, bf16[2,768,768]{2,1,0:T(8,128)(2,1)S(1)}, bf16[2,768,768]{2,1,0:T(8,128)(2,1)S(1)}) custom-call(bf16[196,768]{1,0:T(8,128)(2,1)} %tokens_in.1, bf16[196,768]{1,0:T(8,128)(2,1)} %out_grad_in.1, bf16[768,256]{1,0:T(8,128)(2,1)} %router_in.1, bf16[2,768,768]{2,1,0:T(8,128)(2,1)} %win.1, ...), custom_call_target="tpu_custom_call" | custom-call | tf_op jit(solution)/shard_map/layer/pallas_call | solution.py:515
  118.0 2.3 %store.1 = (bf16[196,768]{1,0:T(8,128)(2,1)}, f32[4,192]{1,0:T(4,128)}, bf16[2,768,768]{2,1,0:T(8,128)(2,1)}, bf16[2,768,768]{2,1,0:T(8,128)(2,1)}) custom-call(bf16[196,768]{1,0:T(8,128)(2,1)S(1)} %get-tuple-element.12.refs_0_, f32[4,192]{1,0:T(4,128)S(1)} %get-tuple-element.13.refs_1_, bf16[2,768,768]{2,1,0:T(8,128)(2,1)S(1)} %get-tuple-element.14.refs_2_, ...), custom_call_target="tpu_custom_call" | custom-call | tf_op jit(solution)/shard_map/store/pallas_call | solution.py:592

commit v8 on v7

--- a/solution.py
+++ b/solution.py
@@ -87,51 +87,51 @@
     ("last", 1),
 )
 EDGE = (
-    (("io", 0, "l", 0), ("io", 1, "l", 0), ("iO", 0, "h", 3), ("iO", 1, "h", 3), ("ix", 0, "h", 2), ("iX", 0, "l", 3), ("ix", 1, "h", 2), ("iX", 1, "l", 3), ("iX", 0, "l", 2)),
-    (("iO", 2, "h", 3), ("io", 3, "l", 0), ("iX", 1, "l", 2), ("iO", 3, "h", 3), ("ix", 2, "h", 2), ("io", 2, "l", 0), ("iX", 2, "l", 3), ("iX", 2, "l", 2), ("iX", 3, "l", 3)),
-    (),
-    (),
-    (("oX", 0, "h", 3), ("oo", 0, "h", 2), ("ix", 3, "h", 2), ("oX", 0, "h", 2), ("iX", 3, "l", 2), ("oo", 0, "h", 0)),
-    (("oo", 0, "h", 1),),
-    (),
-    (("oX", 1, "h", 2), ("oo", 1, "h", 1), ("oo", 1, "h", 0), ("oX", 1, "h", 3)),
-    (),
-    (),
-    (("oX", 2, "h", 3), ("oo", 2, "h", 0)),
-    (("oX", 0, "l", 2), ("oX", 2, "h", 2)),
-    (("oo", 1, "h", 2), ("oo", 2, "h", 1)),
-    (("oT", 0, "h", 2),),
-    (),
-    (),
-    (("oX", 3, "h", 2),),
-    (("oX", 3, "h", 3), ("oX", 1, "l", 2), ("oo", 3, "h", 0)),
-    (("oX", 1, "l", 3), ("oX", 0, "l", 3), ("oT", 1, "h", 2), ("oo", 2, "h", 2), ("oo", 3, "h", 2), ("oX", 2, "l", 2), ("oo", 3, "h", 1), ("oX", 2, "l", 3), ("oX", 3, "l", 2)),
+    (("io", 0, "l", 0), ("iO", 0, "h", 3), ("iO", 1, "h", 3), ("io", 1, "l", 0), ("ix", 0, "h", 2), ("iX", 0, "l", 3), ("iX", 1, "l", 3), ("iX", 0, "l", 2), ("ix", 1, "h", 2)),
+    (("io", 2, "l", 0), ("iO", 2, "h", 3), ("iO", 3, "h", 3), ("iX", 1, "l", 2), ("iX", 2, "l", 3), ("ix", 2, "h", 2), ("iX", 3, "l", 3), ("iX", 2, "l", 2), ("io", 3, "l", 0)),
+    (),
+    (),
+    (("oX", 0, "h", 2), ("ix", 3, "h", 2), ("oX", 0, "h", 3), ("oo", 0, "h", 1), ("oo", 0, "h", 0), ("iX", 3, "l", 2)),
+    (),
+    (),
+    (("oo", 0, "h", 2), ("oX", 1, "h", 3), ("oX", 1, "h", 2), ("oo", 1, "h", 2), ("oo", 1, "h", 1)),
+    (),
+    (),
+    (("oX", 2, "h", 2), ("oX", 2, "h", 3), ("oo", 1, "h", 0)),
+    (),
+    (("oo", 2, "h", 0),),
+    (("oo", 2, "h", 1),),
+    (),
+    (),
+    (("oX", 3, "h", 2), ("oX", 3, "h", 3), ("oX", 0, "l", 2), ("oo", 3, "h", 0), ("oX", 1, "l", 2), ("oX", 0, "l", 3), ("oT", 0, "h", 2), ("oT", 1, "h", 2), ("oo", 3, "h", 1)),
+    (("oo", 3, "h", 2), ("oX", 1, "l", 3)),
+    (("oo", 2, "h", 2), ("oX", 2, "l", 2), ("oX", 2, "l", 3), ("oX", 3, "l", 2)),
     (("oT", 2, "h", 2), ("oX", 3, "l", 3), ("oT", 3, "h", 2)),
     (),
     (),
 )
 INNER = (
-    (("iy", 0, "h", 2), ("iy", 1, "h", 2), ("io", 0, "l", 1), ("io", 0, "l", 0), ("io", 1, "h", 2), ("io", 0, "h", 2), ("io", 1, "l", 0), ("io", 1, "l", 1)),
-    (("io", 0, "h", 1), ("iy", 2, "h", 2), ("iX", 0, "l", 3), ("io", 0, "h", 0), ("iX", 0, "l", 2), ("io", 3, "l", 1), ("iX", 0, "h", 3), ("io", 2, "l", 1), ("iX", 0, "h", 2)),
-    (("iy", 3, "h", 2), ("iX", 1, "l", 2), ("iX", 1, "l", 3)),
-    (("io", 2, "l", 0), ("io", 1, "h", 1), ("iX", 2, "l", 3)),
-    (("iX", 1, "h", 2), ("iX", 2, "l", 2), ("io", 1, "h", 0), ("iX", 1, "h", 3), ("io", 2, "h", 2)),
-    (("io", 3, "l", 0),),
-    (("io", 2, "h", 1), ("oX", 0, "h", 3)),
-    (("io", 2, "h", 0), ("iX", 2, "h", 3), ("iX", 3, "l", 2), ("oX", 0, "h", 2), ("oo", 0, "h", 0), ("iX", 3, "l", 3), ("iX", 2, "h", 2), ("io", 3, "h", 0), ("oX", 0, "l", 2)),
-    (("oX", 1, "h", 2), ("oo", 0, "h", 1)),
-    (("io", 3, "h", 1),),
-    (("iX", 3, "h", 2), ("iX", 3, "h", 3)),
+    (("iy", 0, "h", 2), ("io", 1, "l", 1), ("io", 0, "h", 2), ("iy", 1, "h", 2), ("io", 0, "l", 0), ("io", 0, "l", 1), ("io", 1, "h", 2), ("io", 0, "h", 0)),
+    (("iX", 0, "l", 3), ("iy", 2, "h", 2), ("io", 0, "h", 1), ("iX", 0, "l", 2), ("iX", 0, "h", 3), ("io", 2, "l", 0), ("iX", 0, "h", 2), ("iX", 1, "l", 3), ("io", 1, "h", 1), ("iy", 3, "h", 2), ("iX", 1, "l", 2), ("io", 1, "l", 0), ("iX", 1, "h", 3), ("iX", 2, "l", 2), ("iX", 3, "l", 3), ("iX", 1, "h", 2), ("io", 1, "h", 0), ("iX", 2, "l", 3), ("io", 2, "l", 1)),
+    (),
+    (("iX", 2, "h", 2), ("io", 2, "h", 2), ("io", 3, "l", 1)),
+    (("io", 2, "h", 0),),
+    (("io", 2, "h", 1), ("iX", 2, "h", 3), ("io", 3, "l", 0)),
+    (("oX", 0, "h", 3), ("io", 3, "h", 2), ("oo", 0, "h", 0), ("oX", 0, "h", 2), ("io", 3, "h", 1)),
+    (("iX", 3, "l", 2),),
+    (("iX", 3, "h", 3),),
     (("oX", 1, "h", 3),),
-    (("io", 3, "h", 2), ("oo", 1, "h", 0), ("oX", 2, "h", 3), ("oX", 1, "l", 2)),
-    (("oX", 2, "h", 2), ("oX", 1, "l", 3)),
-    (("oo", 2, "h", 0), ("oX", 0, "l", 3), ("oo", 2, "h", 1), ("oX", 2, "l", 2), ("oo", 1, "h", 1)),
-    (),
-    (),
-    (("oX", 2, "l", 3), ("oX", 3, "h", 2)),
-    (("oo", 0, "l", 0), ("oX", 3, "h", 3), ("oX", 3, "l", 2), ("oo", 3, "h", 0)),
-    (("oX", 3, "l", 3), ("oo", 1, "l", 0)),
-    (("oo", 3, "l", 0), ("oo", 2, "l", 0), ("oo", 3, "h", 1)),
+    (),
+    (("oX", 1, "h", 2),),
+    (),
+    (("io", 3, "h", 0),),
+    (("iX", 3, "h", 2), ("oX", 0, "l", 2), ("oo", 1, "h", 1), ("oX", 1, "l", 2), ("oX", 2, "h", 2)),
+    (("oX", 0, "l", 3), ("oo", 0, "l", 0), ("oo", 0, "h", 1), ("oX", 2, "h", 3)),
+    (("oo", 1, "h", 0), ("oX", 1, "l", 3), ("oX", 3, "h", 2), ("oX", 2, "l", 2), ("oX", 2, "l", 3)),
+    (("oX", 3, "h", 3),),
+    (("oo", 2, "h", 1),),
+    (("oo", 2, "h", 0), ("oX", 3, "l", 2), ("oo", 3, "h", 0), ("oX", 3, "l", 3), ("oo", 1, "l", 0)),
+    (("oo", 2, "l", 0), ("oo", 3, "l", 0), ("oo", 3, "h", 1)),
     (),
 )
 

time: 121 us -> 120 us (level)
  no operation moved by 1% of the time
where the time goes in v8:
time: 120 us
  Pallas kernels  119 us (99%)
    pallas_call x1, Pallas kernels, layer(): pl.pallas_call(exchange_kernel, out_shape=(pltpu.VMEM(tokens.shape, BF),...  117 us

profile of v8, /device:TPU:1, one launch (start us, length us, event | category | flops | bytes accessed | tf_op | source)
XLA Modules:
  0.0 119.9 jit_solution(1502233709067223454)
XLA Ops:
  0.6 116.7 %layer.1 = (bf16[196,768]{1,0:T(8,128)(2,1)S(1)}, f32[4,192]{1,0:T(4,128)S(1)}, bf16[2,768,768]{2,1,0:T(8,128)(2,1)S(1)}, bf16[2,768,768]{2,1,0:T(8,128)(2,1)S(1)}) custom-call(bf16[196,768]{1,0:T(8,128)(2,1)} %tokens_in.1, bf16[196,768]{1,0:T(8,128)(2,1)} %out_grad_in.1, bf16[768,256]{1,0:T(8,128)(2,1)} %router_in.1, bf16[2,768,768]{2,1,0:T(8,128)(2,1)} %win.1, ...), custom_call_target="tpu_custom_call" | custom-call | tf_op jit(solution)/shard_map/layer/pallas_call | solution.py:515
  117.4 2.3 %store.1 = (bf16[196,768]{1,0:T(8,128)(2,1)}, f32[4,192]{1,0:T(4,128)}, bf16[2,768,768]{2,1,0:T(8,128)(2,1)}, bf16[2,768,768]{2,1,0:T(8,128)(2,1)}) custom-call(bf16[196,768]{1,0:T(8,128)(2,1)S(1)} %get-tuple-element.12.refs_0_, f32[4,192]{1,0:T(4,128)S(1)} %get-tuple-element.13.refs_1_, bf16[2,768,768]{2,1,0:T(8,128)(2,1)S(1)} %get-tuple-element.14.refs_2_, ...), custom_call_target="tpu_custom_call" | custom-call | tf_op jit(solution)/shard_map/store/pallas_call | solution.py:592
